TPU v7x, 32 devices: a whole 2x2x4 slice. The times are simulated.
32 devices in a mesh: market: 2 (over y), job: 4 (over z), worker: 4 (over x, core).
Axes of the slice: x: 2, y: 2, z: 4, core: 2. Of those that a mesh axis runs over, the one named last changes fastest.
Arguments:
- worker_feat: bfloat16 [8192, 128], P(('market', 'worker', 'job')), parts along dimension 0, may hold values from -164 to 164
- job_feat: bfloat16 [8192, 128], P(('market', 'job', 'worker')), parts along dimension 0, may hold values from -164 to 164
- affinity: bfloat16 [128, 128], replicated, may hold values from -0.046875 to 0.046875
- worker_mass: float32 [8192], P(('market', 'worker')), parts along dimension 0, may hold values from 0.25 to 4
- job_mass: float32 [8192], P(('market', 'job')), parts along dimension 0, may hold values from 0.25 to 4
- v_start: float32 [8192], P(('market', 'job')), parts along dimension 0, may hold values from -6 to 6
- observed: float32 [256, 128], P('market'), parts along dimension 0, may hold values from -1.5 to 1.5
Outputs:
- gradient: float32 [256, 128], P('market'), parts along dimension 0
- worker_potential: float32 [8192], P(('market', 'worker')), parts along dimension 0
- job_potential: float32 [8192], P(('market', 'job')), parts along dimension 0
There are 2 independent parts, one for each index of `market`. A program takes and returns all parts, laid end to end along the dimension named above; an argument that names none is the same for every part. Nothing has to cross between parts.
All inputs are finite; a program needn't handle non-finite values.
Results may differ from a plain program's by a relative error of at most 0.0003.
The roundings to bfloat16 on the way count: a program that leaves them out, or rounds other values in their place, can miss the bound.
Values may be sent and summed in bfloat16 or wider, within the bound.
No kernel may reach another device: no remote copies, remote signals or barrier semaphores. Data moves between devices by JAX's collectives and lax.ppermute only.
A program may use at most 64 MiB of HBM per device.

v0:
```python
import functools

import jax
import jax.numpy as jnp
from jax import lax
from jax.experimental import pallas as pl
from jax.experimental.pallas import tpu as pltpu
from jax.sharding import PartitionSpec as P


SWEEPS = 3
LANES = 128
TILE = 512
CHUNK = 1024
BY_ROW = (((1,), (1,)), ((), ()))
BY_COLUMN = (((0,), (0,)), ((), ()))
F32 = jnp.float32
BF16 = jnp.bfloat16


def swap(value, axis, size, mask):
    return lax.ppermute(value, axis, [(i, i ^ mask) for i in range(size)])


def widen(value, width):
    return jnp.tile(value, (1, width // LANES))


def merged(pieces):
    highest = functools.reduce(jnp.maximum, pieces)
    return highest + jnp.log(sum(jnp.exp(piece - highest) for piece in pieces))


def new_v(col, pieces):
    cols = col.shape[1]
    both = merged(pieces)
    log_total = both[:, cols : cols + 1]
    return col + log_total - both[:, :cols], log_total


def scores_of(proj_ref, jobs_ref, at):
    return lax.dot_general(
        proj_ref[...], jobs_ref[pl.ds(at, TILE), :], BY_ROW, preferred_element_type=F32
    )


def sweep_rows_and_columns(proj_ref, jobs_ref, v_ref, shift_ref, mass_ref, out_ref, fresh_ref, scratch):
    e_ref, sum_ref, gain_ref = scratch
    rows, cols = proj_ref.shape[0], jobs_ref.shape[0]

    def fast(k, carry):
        at = pl.multiple_of(k * TILE, TILE)
        z = scores_of(proj_ref, jobs_ref, at) + v_ref[:, pl.ds(at, TILE)]
        if shift_ref is not None:
            z = z + widen(shift_ref[...], TILE)
        e = jnp.exp(z)
        e_ref[:, pl.ds(at, TILE)] = e
        part = e[:, :LANES]
        for j in range(1, TILE // LANES):
            part = part + e[:, j * LANES : (j + 1) * LANES]
        sum_ref[...] = sum_ref[...] + part
        return carry

    sum_ref[...] = jnp.zeros_like(sum_ref)
    lax.fori_loop(0, cols // TILE, fast, 0, unroll=True)
    total = jnp.sum(sum_ref[...], axis=1, keepdims=True)
    gain_ref[...] = mass_ref[...] / total
    fresh = jnp.log(gain_ref[...])
    fresh_ref[...] = fresh if shift_ref is None else shift_ref[...] + fresh
    least = jnp.full((1, CHUNK), jnp.inf, F32)
    for k in range(cols // CHUNK):
        span = slice(k * CHUNK, (k + 1) * CHUNK)
        acc = jnp.zeros((8, CHUNK), F32)
        for i in range(rows // 8):
            eight = slice(i * 8, i * 8 + 8)
            acc = acc + e_ref[eight, span] * widen(gain_ref[eight, :], CHUNK)
        column = jnp.sum(acc, axis=0, keepdims=True)
        least = jnp.minimum(least, column)
        out_ref[:, span] = jnp.log(column) - v_ref[:, span]
    safe = (
        (jnp.min(total) > 2.0**-60) & (jnp.max(total) < 2.0**60) & (jnp.min(least) > 2.0**-40)
    )

    @pl.when(jnp.logical_not(safe))
    def _():
        def peak(k, carry):
            at = pl.multiple_of(k * TILE, TILE)
            z = scores_of(proj_ref, jobs_ref, at) + v_ref[:, pl.ds(at, TILE)]
            sum_ref[...] = jnp.maximum(sum_ref[...], jnp.max(z, axis=1, keepdims=True))
            return carry

        sum_ref[...] = jnp.full_like(sum_ref, -jnp.inf)
        lax.fori_loop(0, cols // TILE, peak, 0)
        gain_ref[...] = jnp.zeros_like(gain_ref)

        def add(k, carry):
            at = pl.multiple_of(k * TILE, TILE)
            z = scores_of(proj_ref, jobs_ref, at) + v_ref[:, pl.ds(at, TILE)] - sum_ref[:, :1]
            gain_ref[...] = gain_ref[...] + jnp.sum(jnp.exp(z), axis=1, keepdims=True)
            return carry

        lax.fori_loop(0, cols // TILE, add, 0)
        fresh_ref[...] = jnp.log(mass_ref[...]) - (sum_ref[...] + jnp.log(gain_ref[...]))

        def columns(k, carry):
            at = pl.multiple_of(k * TILE, TILE)
            y = scores_of(proj_ref, jobs_ref, at) + fresh_ref[:, :1]
            top = jnp.max(y, axis=0, keepdims=True)
            out_ref[:, pl.ds(at, TILE)] = top + jnp.log(
                jnp.sum(jnp.exp(y - top), axis=0, keepdims=True)
            )
            return carry

        lax.fori_loop(0, cols // TILE, columns, 0)


def pack_body(workers_hbm, start_hbm, job_mass_hbm, worker_mass_hbm, message_ref, mass_ref, log_total_ref, columns_ref, worker_mass_ref, arrived):
    size, half = workers_hbm.shape[0], start_hbm.shape[0]
    copies = [
        pltpu.make_async_copy(source, target, arrived.at[k])
        for k, (source, target) in enumerate(
            (
                (start_hbm, columns_ref.at[pl.ds(0, half), :]),
                (job_mass_hbm, columns_ref.at[pl.ds(half, half), :]),
                (worker_mass_hbm, worker_mass_ref),
                (workers_hbm, message_ref.at[pl.ds(0, size), :]),
            )
        )
    ]
    for copy in copies:
        copy.start()
    copies[0].wait()
    copies[1].wait()
    rest = columns_ref[...]
    for k in range(3):
        part = rest.astype(BF16)
        message_ref[size + 2 * half * k : size + 2 * half * (k + 1), :] = part
        rest = rest - part.astype(F32)
    copies[2].wait()
    diagonal = diagonal_mask()
    for k in range(worker_mass_ref.shape[0]):
        block = jnp.where(diagonal, worker_mass_ref[k : k + 1, :], 0.0)
        mass_ref[k * LANES : (k + 1) * LANES, :] = jnp.broadcast_to(
            jnp.sum(block, axis=1, keepdims=True), (LANES, LANES)
        )
    log_total_ref[...] = jnp.broadcast_to(
        jnp.log(jnp.sum(worker_mass_ref[...], keepdims=True)), log_total_ref.shape
    )
    copies[3].wait()


def diagonal_mask():
    shape = (LANES, LANES)
    return lax.broadcasted_iota(jnp.int32, shape, 0) == lax.broadcasted_iota(jnp.int32, shape, 1)


def first_body(jobs_n, workers_n, *refs):
    job_pieces, refs = refs[: 3 * jobs_n], refs[3 * jobs_n :]
    messages, refs = refs[:jobs_n], refs[jobs_n:]
    affinity_ref, mass_ref, log_total_ref, *refs = refs
    out_ref, fresh_ref, jobs_ref, workers_ref, proj_ref, col_ref, *refs = refs
    start_ref, *scratch = refs
    job, worker = lax.axis_index("job"), lax.axis_index("worker")
    size = job_pieces[0].shape[0]
    for s in range(jobs_n):
        own, across, other = job_pieces[3 * s : 3 * s + 3]
        for mask, piece in ((0, own[...]), (2, across[...]), (1, other[:size, :]), (3, other[size:, :])):
            at = pl.multiple_of((s * workers_n + (worker ^ mask)) * size, size)
            jobs_ref[pl.ds(at, size), :] = piece
    size = workers_ref.shape[0] // jobs_n
    high = (messages[0].shape[0] - size) // 3
    block = jobs_ref.shape[0] // jobs_n
    for s in range(jobs_n):
        at = pl.multiple_of((job ^ s) * size, size)
        workers_ref[pl.ds(at, size), :] = messages[s][:size, :]
        value = messages[s][size : size + high, :].astype(F32)
        value = value + messages[s][size + high : size + 2 * high, :].astype(F32)
        value = value + messages[s][size + 2 * high :, :].astype(F32)
        for r in range(high // 2):
            lanes = slice(s * block + r * LANES, s * block + (r + 1) * LANES)
            start_ref[:, lanes] = value[r : r + 1, :]
            col_ref[:, lanes] = value[high // 2 + r : high // 2 + r + 1, :]
    col_ref[...] = jnp.log(col_ref[...]) - jnp.log(jnp.sum(col_ref[...], axis=1, keepdims=True))
    proj_ref[...] = jnp.dot(
        workers_ref[...], affinity_ref[...], preferred_element_type=F32
    ).astype(BF16)
    sweep_rows_and_columns(
        proj_ref, jobs_ref, start_ref, None, mass_ref, out_ref, fresh_ref, scratch
    )
    out_ref[:, jobs_ref.shape[0] :] = log_total_ref[...]


def next_body(workers_n, *refs):
    piece_refs, refs = refs[:workers_n], refs[workers_n:]
    proj_ref, jobs_ref, col_ref, shift_ref, mass_ref, log_total_ref, *refs = refs
    out_ref, fresh_ref, v_ref, *scratch = refs
    v_ref[...] = new_v(col_ref[...], [ref[...] for ref in piece_refs])[0]
    sweep_rows_and_columns(
        proj_ref, jobs_ref, v_ref, shift_ref, mass_ref, out_ref, fresh_ref, scratch
    )
    out_ref[:, jobs_ref.shape[0] :] = log_total_ref[...]


def moment_body(workers_n, *refs):
    piece_refs, refs = refs[:workers_n], refs[workers_n:]
    proj_ref, jobs_ref, workers_ref, col_ref, shift_ref, *refs = refs
    moment_ref, u_ref, v_ref, weighted_ref = refs
    rows, cols = proj_ref.shape[0], jobs_ref.shape[0]
    v, log_total = new_v(col_ref[...], [ref[...] for ref in piece_refs])
    v_ref[...] = v
    weighted_ref[...] = jnp.zeros_like(weighted_ref)

    def add(k, carry):
        at = pl.multiple_of(k * TILE, TILE)
        z = scores_of(proj_ref, jobs_ref, at) + widen(shift_ref[...] - log_total, TILE)
        coupling = jnp.exp(z + v_ref[:, pl.ds(at, TILE)]).astype(BF16)
        weighted_ref[...] = weighted_ref[...] + jnp.dot(
            coupling, jobs_ref[pl.ds(at, TILE), :], preferred_element_type=F32
        )
        return carry

    lax.fori_loop(0, cols // TILE, add, 0, unroll=True)
    weighted = weighted_ref[...]
    high = weighted.astype(BF16)
    rest = weighted - high.astype(F32)
    middle = rest.astype(BF16)
    low = (rest - middle.astype(F32)).astype(BF16)
    parts = lax.dot_general(
        workers_ref[...],
        jnp.concatenate([high, middle, low], axis=1),
        BY_COLUMN,
        preferred_element_type=F32,
    )
    wide = high.shape[1]
    moment_ref[...] = parts[:, :wide] + (parts[:, wide : 2 * wide] + parts[:, 2 * wide :])
    u = shift_ref[...] - log_total
    diagonal = diagonal_mask()
    for k in range(rows // LANES):
        block = jnp.where(diagonal, u[k * LANES : (k + 1) * LANES, :], 0.0)
        u_ref[:, k * LANES : (k + 1) * LANES] = jnp.sum(block, axis=0, keepdims=True)


def call(body, outs, n_in, scratch):
    vmem = pl.BlockSpec(memory_space=pltpu.VMEM)
    return pl.pallas_call(
        body,
        out_shape=tuple(jax.ShapeDtypeStruct(shape, dtype) for shape, dtype in outs),
        in_specs=[vmem] * n_in,
        out_specs=(vmem,) * len(outs),
        scratch_shapes=[pltpu.VMEM(shape, F32) for shape in scratch],
        compiler_params=pltpu.CompilerParams(vmem_limit_bytes=40 << 20),
    )


def replicated_plan(jobs_n, workers_n):
    def over_job(value):
        return [value] + [swap(value, "job", jobs_n, s) for s in range(1, jobs_n)]

    def over_worker(value):
        return [value] + [swap(value, "worker", workers_n, s) for s in range(1, workers_n)]

    def on_device(worker_feat, job_feat, affinity, worker_mass, job_mass, v_start, observed):
        rows, cols = jobs_n * worker_feat.shape[0], jobs_n * workers_n * job_feat.shape[0]
        feat = worker_feat.shape[1]
        own_rows, own_cols = worker_feat.shape[0], cols // jobs_n
        high = 2 * (own_cols // LANES)
        wide, tall = ((1, cols + LANES), F32), ((rows, LANES), F32)
        vmem, anywhere = pl.BlockSpec(memory_space=pltpu.VMEM), pl.BlockSpec(memory_space=pl.ANY)
        message, mass, log_total = pl.pallas_call(
            pack_body,
            out_shape=(
                jax.ShapeDtypeStruct((own_rows + 3 * high, feat), BF16),
                jax.ShapeDtypeStruct((rows, LANES), F32),
                jax.ShapeDtypeStruct((1, LANES), F32),
            ),
            in_specs=[anywhere] * 4,
            out_specs=(vmem,) * 3,
            scratch_shapes=[
                pltpu.VMEM((high, LANES), F32),
                pltpu.VMEM((rows // LANES, LANES), F32),
                pltpu.SemaphoreType.DMA((4,)),
            ],
            compiler_params=pltpu.CompilerParams(vmem_limit_bytes=8 << 20),
            name="pack",
        )(
            worker_feat,
            v_start.reshape(-1, LANES),
            job_mass.reshape(-1, LANES),
            worker_mass.reshape(-1, LANES),
        )
        job_pieces = []
        for own in over_job(job_feat):
            across = swap(own, "worker", workers_n, 2)
            both = jnp.concatenate([own, across], axis=0)
            other = swap(both, "worker", workers_n, 1)
            job_pieces += [own, across, other]
        messages = over_job(message)
        work = [(rows, cols), (rows, LANES), (rows, LANES)]
        out, shift, jobs, workers, proj, log_job = call(
            functools.partial(first_body, jobs_n, workers_n),
            [
                wide,
                tall,
                ((cols, feat), BF16),
                ((rows, feat), BF16),
                ((rows, feat), BF16),
                ((1, cols), F32),
            ],
            4 * jobs_n + 3,
            [(1, cols)] + work,
        )(*job_pieces, *messages, affinity, mass, log_total)
        for _ in range(1, SWEEPS):
            out, shift = call(
                functools.partial(next_body, workers_n),
                [wide, tall],
                workers_n + 6,
                [(1, cols)] + work,
            )(*over_worker(out), proj, jobs, log_job, shift, mass, log_total)
        moment, pot_u, pot_v = call(
            functools.partial(moment_body, workers_n),
            [((feat, feat), F32), ((1, rows), F32), ((1, cols), F32)],
            workers_n + 5,
            [(rows, feat)],
        )(*over_worker(out), proj, jobs, workers, log_job, shift)
        moment = sum(over_worker(moment))
        own_jobs = cols // jobs_n
        return (moment - observed, pot_u.reshape(rows), pot_v[0, :own_jobs])

    return on_device


def tiled_plan(jobs_n, workers_n):
    def parts_of(value, axis, size):
        if size & (size - 1) or size > 8:
            gathered = lax.all_gather(value, axis)
            return [gathered[k] for k in range(size)]
        return [value] + [swap(value, axis, size, mask) for mask in range(1, size)]

    def local_lse(scores, axis):
        highest = jnp.max(scores, axis=axis, keepdims=True)
        return jnp.squeeze(highest, axis) + jnp.log(jnp.sum(jnp.exp(scores - highest), axis=axis))

    def on_device(worker_feat, job_feat, affinity, worker_mass, job_mass, v_start, observed):
        jobs_local = lax.all_gather(job_feat, "worker", axis=0, tiled=True)
        workers_local = lax.all_gather(worker_feat, "job", axis=0, tiled=True)
        projected = jnp.dot(workers_local, affinity, preferred_element_type=F32).astype(BF16)
        worker_sum = sum(parts_of(jnp.sum(worker_mass).reshape(1, 1), "worker", workers_n))
        job_sum = sum(parts_of(jnp.sum(job_mass).reshape(1, 1), "job", jobs_n))
        log_worker = jnp.log(worker_mass) - jnp.log(worker_sum[0])
        log_job = jnp.log(job_mass) - jnp.log(job_sum[0])
        tile = lax.dot_general(projected, jobs_local, BY_ROW, preferred_element_type=F32)
        pot_v = v_start
        pot_u = log_worker
        for _ in range(SWEEPS):
            rows = local_lse(tile + pot_v[None, :], 1)
            pot_u = log_worker - merged(parts_of(rows, "job", jobs_n))
            columns = local_lse(tile + pot_u[:, None], 0)
            pot_v = log_job - merged(parts_of(columns, "worker", workers_n))
        coupling = jnp.exp(tile + pot_u[:, None] + pot_v[None, :]).astype(BF16)
        weighted = jnp.dot(coupling, jobs_local, preferred_element_type=F32)
        moment = lax.dot_general(
            workers_local.astype(F32), weighted, BY_COLUMN, precision=lax.Precision.HIGHEST
        )
        moment = sum(parts_of(sum(parts_of(moment, "worker", workers_n)), "job", jobs_n))
        return (moment - observed, pot_u, pot_v)

    return on_device


def solution(mesh):
    placed = (
        P(("market", "worker", "job"), None),
        P(("market", "job", "worker"), None),
        P(),
        P(("market", "worker")),
        P(("market", "job")),
        P(("market", "job")),
        P("market", None),
    )
    jobs_n, workers_n = mesh.shape["job"], mesh.shape["worker"]
    replicated = (jobs_n, workers_n) == (4, 4)
    plan = replicated_plan if replicated else tiled_plan

    def layered(*args):
        return plan(jobs_n, workers_n)(*args)

    return jax.shard_map(
        layered,
        mesh=mesh,
        in_specs=placed,
        out_specs=(P("market", None), P(("market", "worker")), P(("market", "job"))),
        check_vma=False,
    )
```

profile of v0, /device:TPU:0, one launch (start us, length us, event | category | flops | bytes accessed | tf_op | source)
XLA Modules:
  0.0 115.1 jit_solution(13094781349235353683)
XLA Ops:
  0.6 4.1 %collective-permute-start.5 = (bf16[256,128]{1,0:T(8,128)(2,1)}, bf16[256,128]{1,0:T(8,128)(2,1)S(1)}, u32[]{:S(2)}, u32[]{:S(2)}) collective-permute-start(bf16[256,128]{1,0:T(8,128)(2,1)} %refs_0_.1), channel_id=1, source_target_pairs={{0,8},{4,12},{8,0},{12,4},{1,9},{5,13},{9,1},{13,5},{2,10},{6,14},... | collective-permute-start | bytes 196616 | tf_op jit(solution)/shard_map/ppermute | solution.py:22
  4.8 1.5 %collective-permute-start = (bf16[256,128]{1,0:T(8,128)(2,1)}, bf16[256,128]{1,0:T(8,128)(2,1)S(1)}, u32[]{:S(2)}, u32[]{:S(2)}) collective-permute-start(bf16[256,128]{1,0:T(8,128)(2,1)} %refs_0_.1), channel_id=1, source_target_pairs={{0,2},{1,3},{2,0},{3,1},{4,6},{5,7},{6,4},{7,5},{8,10},{9,11},{10,... | collective-permute-start | bytes 196616 | tf_op jit(solution)/shard_map/ppermute | solution.py:22
  6.3 1.6 %collective-permute-start.2 = (bf16[256,128]{1,0:T(8,128)(2,1)}, bf16[256,128]{1,0:T(8,128)(2,1)S(1)}, u32[]{:S(2)}, u32[]{:S(2)}) collective-permute-start(bf16[256,128]{1,0:T(8,128)(2,1)} %refs_0_.1), channel_id=1, source_target_pairs={{0,4},{4,0},{8,12},{12,8},{1,5},{5,1},{9,13},{13,9},{2,6},{6,2},{1... | collective-permute-start | bytes 196616 | tf_op jit(solution)/shard_map/ppermute | solution.py:22
  7.8 0.2 collective-permute-start.8
  8.1 0.8 copy-done.1
  8.9 0.7 copy-done.3
  9.6 0.7 copy-done.4
  10.3 0.7 copy-done.5
  11.0 0.3 pack.1
  11.3 3.7 %collective-permute-start.13 = (bf16[304,128]{1,0:T(8,128)(2,1)S(1)}, bf16[304,128]{1,0:T(8,128)(2,1)S(1)}, u32[]{:S(2)}, u32[]{:S(2)}) collective-permute-start(bf16[304,128]{1,0:T(8,128)(2,1)S(1)} %get-tuple-element.19.refs_12_), channel_id=1, source_target_pairs={{0,12},{4,8},{8,4},{12,0},{1,13},{5,9},{9,5},{13,1},{2,14},{6,10},... | collective-permute-start | bytes 233480 | tf_op jit(solution)/shard_map/ppermute | solution.py:22
  15.0 0.6 collective-permute-start.6
  15.6 0.0 collective-permute-done.2.refs_3_
  15.6 0.1 collective-permute-start.1
  15.7 1.6 %collective-permute-start.3 = (bf16[256,128]{1,0:T(8,128)(2,1)S(1)}, bf16[256,128]{1,0:T(8,128)(2,1)S(1)}, u32[]{:S(2)}, u32[]{:S(2)}) collective-permute-start(bf16[256,128]{1,0:T(8,128)(2,1)S(1)} %collective-permute-done.2.refs_3_), channel_id=1, source_target_pairs={{0,2},{1,3},{2,0},{3,1},{4,6},{5,7},{6,4},{7,5},{8,10},{9,11},{10,... | collective-permute-start | bytes 196616 | tf_op jit(solution)/shard_map/ppermute | solution.py:22
  17.3 2.6 %collective-permute-done.6.refs_7_ = bf16[256,128]{1,0:T(8,128)(2,1)S(1)} collective-permute-done((bf16[256,128]{1,0:T(8,128)(2,1)S(1)}, bf16[256,128]{1,0:T(8,128)(2,1)S(1)}, u32[]{:S(2)}, u32[]{:S(2)}) %collective-permute-start.6) | collective-permute-done | bytes 65568 | tf_op jit(solution)/shard_map/ppermute | solution.py:22
  19.9 0.0 collective-permute-start.9
  19.9 1.4 %collective-permute-done.3.refs_4_ = bf16[256,128]{1,0:T(8,128)(2,1)S(1)} collective-permute-done((bf16[256,128]{1,0:T(8,128)(2,1)S(1)}, bf16[256,128]{1,0:T(8,128)(2,1)S(1)}, u32[]{:S(2)}, u32[]{:S(2)}) %collective-permute-start.3) | collective-permute-done | bytes 65568 | tf_op jit(solution)/shard_map/ppermute | solution.py:22
  21.3 0.0 copy-start.2
  21.3 2.8 %collective-permute-done.9.refs_10_ = bf16[256,128]{1,0:T(8,128)(2,1)S(1)} collective-permute-done((bf16[256,128]{1,0:T(8,128)(2,1)S(1)}, bf16[256,128]{1,0:T(8,128)(2,1)S(1)}, u32[]{:S(2)}, u32[]{:S(2)}) %collective-permute-start.9) | collective-permute-done | bytes 65568 | tf_op jit(solution)/shard_map/ppermute | solution.py:22
  24.1 0.6 collective-permute-start.10
  24.7 0.9 collective-permute-start.11
  25.6 3.5 %collective-permute-done.11.refs_13_ = bf16[304,128]{1,0:T(8,128)(2,1)S(1)} collective-permute-done((bf16[304,128]{1,0:T(8,128)(2,1)S(1)}, bf16[304,128]{1,0:T(8,128)(2,1)S(1)}, u32[]{:S(2)}, u32[]{:S(2)}) %collective-permute-start.11) | collective-permute-done | bytes 77856 | tf_op jit(solution)/shard_map/ppermute | solution.py:22
  29.2 20.5 %shard_map.94 = (f32[1,4224]{1,0:T(1,128)S(1)}, f32[1024,128]{1,0:T(8,128)S(1)}, bf16[4096,128]{1,0:T(8,128)(2,1)S(1)}, bf16[1024,128]{1,0:T(8,128)(2,1)S(1)}, b...) custom-call(bf16[256,128]{1,0:T(8,128)(2,1)S(1)} %copy-done, bf16[256,128]{1,0:T(8,128)(2,1)S(1)} %collective-permute-done.refs_1_, ...), custom_call_target="tpu_custom_call" | custom-call | tf_op jit(solution)/shard_map/pallas_call | solution.py:299
  49.7 0.1 collective-permute-start.16
  49.7 0.6 collective-permute-start.15
  50.3 1.3 %collective-permute-start.14 = (f32[1,4224]{1,0:T(1,128)S(1)}, f32[1,4224]{1,0:T(1,128)S(1)}, u32[]{:S(2)}, u32[]{:S(2)}) collective-permute-start(f32[1,4224]{1,0:T(1,128)S(1)} %get-tuple-element.22.refs_0_), channel_id=1, source_target_pairs={{0,1},{1,0},{2,3},{3,2},{4,5},{5,4},{6,7},{7,6},{8,9},{9,8},{10,11... | collective-permute-start | bytes 50696 | tf_op jit(solution)/shard_map/ppermute | solution.py:22
  51.6 1.3 %collective-permute-done.16.refs_3_ = f32[1,4224]{1,0:T(1,128)S(1)} collective-permute-done((f32[1,4224]{1,0:T(1,128)S(1)}, f32[1,4224]{1,0:T(1,128)S(1)}, u32[]{:S(2)}, u32[]{:S(2)}) %collective-permute-start.16) | collective-permute-done | bytes 16928 | tf_op jit(solution)/shard_map/ppermute | solution.py:22
  52.9 0.7 collective-permute-done.15.refs_2_
  53.6 20.8 %shard_map.95 = (f32[1,4224]{1,0:T(1,128)S(1)}, f32[1024,128]{1,0:T(8,128)S(1)}) custom-call(f32[1,4224]{1,0:T(1,128)S(1)} %get-tuple-element.22.refs_0_, f32[1,4224]{1,0:T(1,128)S(1)} %collective-permute-done.14.refs_1_, f32[1,4224]{1,0:T(1,128)S(1)} %collective-permute-done.15.refs_2_, f32[1,4224]{1,0:T(1,128)S(1)} %collective-permute-done.16.refs_3_, ...), custom_call_target="tpu_custom_call" | custom-call | tf_op jit(solution)/shard_map/pallas_call | solution.py:313
  74.4 0.6 collective-permute-start.19
  74.9 0.6 collective-permute-start.18
  75.5 0.8 collective-permute-start.17
  76.3 1.3 %collective-permute-done.19.refs_3_ = f32[1,4224]{1,0:T(1,128)S(1)} collective-permute-done((f32[1,4224]{1,0:T(1,128)S(1)}, f32[1,4224]{1,0:T(1,128)S(1)}, u32[]{:S(2)}, u32[]{:S(2)}) %collective-permute-start.19) | collective-permute-done | bytes 16928 | tf_op jit(solution)/shard_map/ppermute | solution.py:22
  77.6 1.1 collective-permute-done.18.refs_2_
  78.7 21.1 %shard_map.96 = (f32[1,4224]{1,0:T(1,128)S(1)}, f32[1024,128]{1,0:T(8,128)S(1)}) custom-call(f32[1,4224]{1,0:T(1,128)S(1)} %get-tuple-element.27.refs_0_, f32[1,4224]{1,0:T(1,128)S(1)} %collective-permute-done.17.refs_1_, f32[1,4224]{1,0:T(1,128)S(1)} %collective-permute-done.18.refs_2_, f32[1,4224]{1,0:T(1,128)S(1)} %collective-permute-done.19.refs_3_, ...), custom_call_target="tpu_custom_call" | custom-call | tf_op jit(solution)/shard_map/pallas_call | solution.py:313
  99.8 0.5 collective-permute-start.22
  100.2 0.4 collective-permute-start.21
  100.6 1.1 collective-permute-start.20
  101.7 1.3 %collective-permute-done.22.refs_3_ = f32[1,4224]{1,0:T(1,128)S(1)} collective-permute-done((f32[1,4224]{1,0:T(1,128)S(1)}, f32[1,4224]{1,0:T(1,128)S(1)}, u32[]{:S(2)}, u32[]{:S(2)}) %collective-permute-start.22) | collective-permute-done | bytes 16928 | tf_op jit(solution)/shard_map/ppermute | solution.py:22
  103.0 1.0 collective-permute-done.21.refs_2_
  104.0 5.3 %shard_map.97 = (f32[128,128]{1,0:T(8,128)S(1)}, f32[1,1024]{1,0:T(1,128)}, f32[1,4096]{1,0:T(1,128)S(1)}) custom-call(f32[1,4224]{1,0:T(1,128)S(1)} %get-tuple-element.29.refs_0_, f32[1,4224]{1,0:T(1,128)S(1)} %collective-permute-done.20.refs_1_, f32[1,4224]{1,0:T(1,128)S(1)} %collective-permute-done.21.refs_2_, ...), custom_call_target="tpu_custom_call" | custom-call | tf_op jit(solution)/shard_map/pallas_call | solution.py:319
  109.3 0.2 collective-permute-start.25
  109.5 0.7 collective-permute-start.24
  110.2 1.0 collective-permute-start.23
  111.2 0.6 slice.3
  111.8 1.4 %collective-permute-done.25 = f32[128,128]{1,0:T(8,128)S(1)} collective-permute-done((f32[128,128]{1,0:T(8,128)S(1)}, f32[128,128]{1,0:T(8,128)S(1)}, u32[]{:S(2)}, u32[]{:S(2)}) %collective-permute-start.25) | collective-permute-done | bytes 65568 | tf_op jit(solution)/shard_map/ppermute | solution.py:22
  113.1 1.3 %collective-permute-done.24 = f32[128,128]{1,0:T(8,128)S(1)} collective-permute-done((f32[128,128]{1,0:T(8,128)S(1)}, f32[128,128]{1,0:T(8,128)S(1)}, u32[]{:S(2)}, u32[]{:S(2)}) %collective-permute-start.24) | collective-permute-done | bytes 65568 | tf_op jit(solution)/shard_map/ppermute | solution.py:22
  114.5 0.7 add_subtract_fusion
  (29 shorter events, 0.1 us)
Async XLA Ops:
  0.6 15.0 %copy-start = (bf16[256,128]{1,0:T(8,128)(2,1)S(1)}, bf16[256,128]{1,0:T(8,128)(2,1)}, u32[]{:S(2)}) copy-start(bf16[256,128]{1,0:T(8,128)(2,1)} %refs_0_.1) | copy-start | bytes 196612
  0.6 14.3 %collective-permute-start.5 = (bf16[256,128]{1,0:T(8,128)(2,1)}, bf16[256,128]{1,0:T(8,128)(2,1)S(1)}, u32[]{:S(2)}, u32[]{:S(2)}) collective-permute-start(bf16[256,128]{1,0:T(8,128)(2,1)} %refs_0_.1), channel_id=1, source_target_pairs={{0,8},{4,12},{8,0},{12,4},{1,9},{5,13},{9,1},{13,5},{2,10},{6,14},... | collective-permute-start | bytes 196616 | tf_op jit(solution)/shard_map/ppermute | solution.py:22
  4.8 10.2 %collective-permute-start = (bf16[256,128]{1,0:T(8,128)(2,1)}, bf16[256,128]{1,0:T(8,128)(2,1)S(1)}, u32[]{:S(2)}, u32[]{:S(2)}) collective-permute-start(bf16[256,128]{1,0:T(8,128)(2,1)} %refs_0_.1), channel_id=1, source_target_pairs={{0,2},{1,3},{2,0},{3,1},{4,6},{5,7},{6,4},{7,5},{8,10},{9,11},{10,... | collective-permute-start | bytes 196616 | tf_op jit(solution)/shard_map/ppermute | solution.py:22
  6.3 9.4 %collective-permute-start.2 = (bf16[256,128]{1,0:T(8,128)(2,1)}, bf16[256,128]{1,0:T(8,128)(2,1)S(1)}, u32[]{:S(2)}, u32[]{:S(2)}) collective-permute-start(bf16[256,128]{1,0:T(8,128)(2,1)} %refs_0_.1), channel_id=1, source_target_pairs={{0,4},{4,0},{8,12},{12,8},{1,5},{5,1},{9,13},{13,9},{2,6},{6,2},{1... | collective-permute-start | bytes 196616 | tf_op jit(solution)/shard_map/ppermute | solution.py:22
  7.8 7.9 %collective-permute-start.8 = (bf16[256,128]{1,0:T(8,128)(2,1)}, bf16[256,128]{1,0:T(8,128)(2,1)S(1)}, u32[]{:S(2)}, u32[]{:S(2)}) collective-permute-start(bf16[256,128]{1,0:T(8,128)(2,1)} %refs_0_.1), channel_id=1, source_target_pairs={{0,12},{4,8},{8,4},{12,0},{1,13},{5,9},{9,5},{13,1},{2,14},{6,10},... | collective-permute-start | bytes 196616 | tf_op jit(solution)/shard_map/ppermute | solution.py:22
  8.1 0.8 copy-start.1
  8.9 0.7 copy-start.3
  9.6 0.7 copy-start.4
  10.3 0.7 copy-start.5
  11.3 12.8 %collective-permute-start.13 = (bf16[304,128]{1,0:T(8,128)(2,1)S(1)}, bf16[304,128]{1,0:T(8,128)(2,1)S(1)}, u32[]{:S(2)}, u32[]{:S(2)}) collective-permute-start(bf16[304,128]{1,0:T(8,128)(2,1)S(1)} %get-tuple-element.19.refs_12_), channel_id=1, source_target_pairs={{0,12},{4,8},{8,4},{12,0},{1,13},{5,9},{9,5},{13,1},{2,14},{6,10},... | collective-permute-start | bytes 233480 | tf_op jit(solution)/shard_map/ppermute | solution.py:22
  15.0 9.7 %collective-permute-start.12 = (bf16[304,128]{1,0:T(8,128)(2,1)S(1)}, bf16[304,128]{1,0:T(8,128)(2,1)S(1)}, u32[]{:S(2)}, u32[]{:S(2)}) collective-permute-start(bf16[304,128]{1,0:T(8,128)(2,1)S(1)} %get-tuple-element.19.refs_12_), channel_id=1, source_target_pairs={{0,8},{4,12},{8,0},{12,4},{1,9},{5,13},{9,1},{13,5},{2,10},{6,14},... | collective-permute-start | bytes 233480 | tf_op jit(solution)/shard_map/ppermute | solution.py:22
  15.0 4.9 %collective-permute-start.6 = (bf16[256,128]{1,0:T(8,128)(2,1)S(1)}, bf16[256,128]{1,0:T(8,128)(2,1)S(1)}, u32[]{:S(2)}, u32[]{:S(2)}) collective-permute-start(bf16[256,128]{1,0:T(8,128)(2,1)S(1)} %collective-permute-done.5.refs_6_), channel_id=1, source_target_pairs={{0,2},{1,3},{2,0},{3,1},{4,6},{5,7},{6,4},{7,5},{8,10},{9,11},{10,... | collective-permute-start | bytes 196616 | tf_op jit(solution)/shard_map/ppermute | solution.py:22
  15.6 13.5 %collective-permute-start.1 = (bf16[512,128]{1,0:T(8,128)(2,1)S(1)}, bf16[512,128]{1,0:T(8,128)(2,1)S(1)}, u32[]{:S(2)}, u32[]{:S(2)}) collective-permute-start(bf16[512,128]{1,0:T(8,128)(2,1)S(1)} %pad_maximum_fusion), channel_id=1, source_target_pairs={{0,1},{1,0},{2,3},{3,2},{4,5},{5,4},{6,7},{7,6},{8,9},{9,8},{10,11... | collective-permute-start | bytes 393224 | tf_op jit(solution)/shard_map/ppermute | solution.py:22
  15.7 5.5 %collective-permute-start.3 = (bf16[256,128]{1,0:T(8,128)(2,1)S(1)}, bf16[256,128]{1,0:T(8,128)(2,1)S(1)}, u32[]{:S(2)}, u32[]{:S(2)}) collective-permute-start(bf16[256,128]{1,0:T(8,128)(2,1)S(1)} %collective-permute-done.2.refs_3_), channel_id=1, source_target_pairs={{0,2},{1,3},{2,0},{3,1},{4,6},{5,7},{6,4},{7,5},{8,10},{9,11},{10,... | collective-permute-start | bytes 196616 | tf_op jit(solution)/shard_map/ppermute | solution.py:22
  19.9 4.3 %collective-permute-start.9 = (bf16[256,128]{1,0:T(8,128)(2,1)S(1)}, bf16[256,128]{1,0:T(8,128)(2,1)S(1)}, u32[]{:S(2)}, u32[]{:S(2)}) collective-permute-start(bf16[256,128]{1,0:T(8,128)(2,1)S(1)} %collective-permute-done.8.refs_9_), channel_id=1, source_target_pairs={{0,2},{1,3},{2,0},{3,1},{4,6},{5,7},{6,4},{7,5},{8,10},{9,11},{10,... | collective-permute-start | bytes 196616 | tf_op jit(solution)/shard_map/ppermute | solution.py:22
  21.3 7.9 %collective-permute-start.7 = (bf16[512,128]{1,0:T(8,128)(2,1)S(1)}, bf16[512,128]{1,0:T(8,128)(2,1)S(1)}, u32[]{:S(2)}, u32[]{:S(2)}) collective-permute-start(bf16[512,128]{1,0:T(8,128)(2,1)S(1)} %pad_maximum_fusion.2), channel_id=1, source_target_pairs={{0,1},{1,0},{2,3},{3,2},{4,5},{5,4},{6,7},{7,6},{8,9},{9,8},{10,11... | collective-permute-start | bytes 393224 | tf_op jit(solution)/shard_map/ppermute | solution.py:22
  21.3 7.9 %copy-start.2 = (bf16[128,128]{1,0:T(8,128)(2,1)S(1)}, bf16[128,128]{1,0:T(8,128)(2,1)}, u32[]{:S(2)}) copy-start(bf16[128,128]{1,0:T(8,128)(2,1)} %refs_16_.1) | copy-start | bytes 98308
  24.1 5.0 %collective-permute-start.4 = (bf16[512,128]{1,0:T(8,128)(2,1)S(1)}, bf16[512,128]{1,0:T(8,128)(2,1)S(1)}, u32[]{:S(2)}, u32[]{:S(2)}) collective-permute-start(bf16[512,128]{1,0:T(8,128)(2,1)S(1)} %pad_maximum_fusion.1), channel_id=1, source_target_pairs={{0,1},{1,0},{2,3},{3,2},{4,5},{5,4},{6,7},{7,6},{8,9},{9,8},{10,11... | collective-permute-start | bytes 393224 | tf_op jit(solution)/shard_map/ppermute | solution.py:22
  24.1 5.0 %collective-permute-start.10 = (bf16[512,128]{1,0:T(8,128)(2,1)S(1)}, bf16[512,128]{1,0:T(8,128)(2,1)S(1)}, u32[]{:S(2)}, u32[]{:S(2)}) collective-permute-start(bf16[512,128]{1,0:T(8,128)(2,1)S(1)} %pad_maximum_fusion.3), channel_id=1, source_target_pairs={{0,1},{1,0},{2,3},{3,2},{4,5},{5,4},{6,7},{7,6},{8,9},{9,8},{10,11... | collective-permute-start | bytes 393224 | tf_op jit(solution)/shard_map/ppermute | solution.py:22
  24.7 4.4 %collective-permute-start.11 = (bf16[304,128]{1,0:T(8,128)(2,1)S(1)}, bf16[304,128]{1,0:T(8,128)(2,1)S(1)}, u32[]{:S(2)}, u32[]{:S(2)}) collective-permute-start(bf16[304,128]{1,0:T(8,128)(2,1)S(1)} %get-tuple-element.19.refs_12_), channel_id=1, source_target_pairs={{0,4},{4,0},{8,12},{12,8},{1,5},{5,1},{9,13},{13,9},{2,6},{6,2},{1... | collective-permute-start | bytes 233480 | tf_op jit(solution)/shard_map/ppermute | solution.py:22
  49.7 3.2 %collective-permute-start.16 = (f32[1,4224]{1,0:T(1,128)S(1)}, f32[1,4224]{1,0:T(1,128)S(1)}, u32[]{:S(2)}, u32[]{:S(2)}) collective-permute-start(f32[1,4224]{1,0:T(1,128)S(1)} %get-tuple-element.22.refs_0_), channel_id=1, source_target_pairs={{0,3},{1,2},{2,1},{3,0},{4,7},{5,6},{6,5},{7,4},{8,11},{9,10},{10,... | collective-permute-start | bytes 50696 | tf_op jit(solution)/shard_map/ppermute | solution.py:22
  49.7 3.8 %collective-permute-start.15 = (f32[1,4224]{1,0:T(1,128)S(1)}, f32[1,4224]{1,0:T(1,128)S(1)}, u32[]{:S(2)}, u32[]{:S(2)}) collective-permute-start(f32[1,4224]{1,0:T(1,128)S(1)} %get-tuple-element.22.refs_0_), channel_id=1, source_target_pairs={{0,2},{1,3},{2,0},{3,1},{4,6},{5,7},{6,4},{7,5},{8,10},{9,11},{10,... | collective-permute-start | bytes 50696 | tf_op jit(solution)/shard_map/ppermute | solution.py:22
  50.3 3.3 %collective-permute-start.14 = (f32[1,4224]{1,0:T(1,128)S(1)}, f32[1,4224]{1,0:T(1,128)S(1)}, u32[]{:S(2)}, u32[]{:S(2)}) collective-permute-start(f32[1,4224]{1,0:T(1,128)S(1)} %get-tuple-element.22.refs_0_), channel_id=1, source_target_pairs={{0,1},{1,0},{2,3},{3,2},{4,5},{5,4},{6,7},{7,6},{8,9},{9,8},{10,11... | collective-permute-start | bytes 50696 | tf_op jit(solution)/shard_map/ppermute | solution.py:22
  74.4 3.2 %collective-permute-start.19 = (f32[1,4224]{1,0:T(1,128)S(1)}, f32[1,4224]{1,0:T(1,128)S(1)}, u32[]{:S(2)}, u32[]{:S(2)}) collective-permute-start(f32[1,4224]{1,0:T(1,128)S(1)} %get-tuple-element.27.refs_0_), channel_id=1, source_target_pairs={{0,3},{1,2},{2,1},{3,0},{4,7},{5,6},{6,5},{7,4},{8,11},{9,10},{10,... | collective-permute-start | bytes 50696 | tf_op jit(solution)/shard_map/ppermute | solution.py:22
  74.9 3.7 %collective-permute-start.18 = (f32[1,4224]{1,0:T(1,128)S(1)}, f32[1,4224]{1,0:T(1,128)S(1)}, u32[]{:S(2)}, u32[]{:S(2)}) collective-permute-start(f32[1,4224]{1,0:T(1,128)S(1)} %get-tuple-element.27.refs_0_), channel_id=1, source_target_pairs={{0,2},{1,3},{2,0},{3,1},{4,6},{5,7},{6,4},{7,5},{8,10},{9,11},{10,... | collective-permute-start | bytes 50696 | tf_op jit(solution)/shard_map/ppermute | solution.py:22
  75.5 3.2 %collective-permute-start.17 = (f32[1,4224]{1,0:T(1,128)S(1)}, f32[1,4224]{1,0:T(1,128)S(1)}, u32[]{:S(2)}, u32[]{:S(2)}) collective-permute-start(f32[1,4224]{1,0:T(1,128)S(1)} %get-tuple-element.27.refs_0_), channel_id=1, source_target_pairs={{0,1},{1,0},{2,3},{3,2},{4,5},{5,4},{6,7},{7,6},{8,9},{9,8},{10,11... | collective-permute-start | bytes 50696 | tf_op jit(solution)/shard_map/ppermute | solution.py:22
  99.8 3.2 %collective-permute-start.22 = (f32[1,4224]{1,0:T(1,128)S(1)}, f32[1,4224]{1,0:T(1,128)S(1)}, u32[]{:S(2)}, u32[]{:S(2)}) collective-permute-start(f32[1,4224]{1,0:T(1,128)S(1)} %get-tuple-element.29.refs_0_), channel_id=1, source_target_pairs={{0,3},{1,2},{2,1},{3,0},{4,7},{5,6},{6,5},{7,4},{8,11},{9,10},{10,... | collective-permute-start | bytes 50696 | tf_op jit(solution)/shard_map/ppermute | solution.py:22
  100.2 3.7 %collective-permute-start.21 = (f32[1,4224]{1,0:T(1,128)S(1)}, f32[1,4224]{1,0:T(1,128)S(1)}, u32[]{:S(2)}, u32[]{:S(2)}) collective-permute-start(f32[1,4224]{1,0:T(1,128)S(1)} %get-tuple-element.29.refs_0_), channel_id=1, source_target_pairs={{0,2},{1,3},{2,0},{3,1},{4,6},{5,7},{6,4},{7,5},{8,10},{9,11},{10,... | collective-permute-start | bytes 50696 | tf_op jit(solution)/shard_map/ppermute | solution.py:22
  100.6 3.4 %collective-permute-start.20 = (f32[1,4224]{1,0:T(1,128)S(1)}, f32[1,4224]{1,0:T(1,128)S(1)}, u32[]{:S(2)}, u32[]{:S(2)}) collective-permute-start(f32[1,4224]{1,0:T(1,128)S(1)} %get-tuple-element.29.refs_0_), channel_id=1, source_target_pairs={{0,1},{1,0},{2,3},{3,2},{4,5},{5,4},{6,7},{7,6},{8,9},{9,8},{10,11... | collective-permute-start | bytes 50696 | tf_op jit(solution)/shard_map/ppermute | solution.py:22
  104.0 10.5 %copy-start.6 = (f32[128,128]{1,0:T(8,128)S(1)}, f32[128,128]{1,0:T(8,128)}, u32[]{:S(2)}) copy-start(f32[128,128]{1,0:T(8,128)} %param.13) | copy-start | bytes 196612
  109.3 3.8 %collective-permute-start.25 = (f32[128,128]{1,0:T(8,128)S(1)}, f32[128,128]{1,0:T(8,128)S(1)}, u32[]{:S(2)}, u32[]{:S(2)}) collective-permute-start(f32[128,128]{1,0:T(8,128)S(1)} %get-tuple-element.32), channel_id=1, source_target_pairs={{0,3},{1,2},{2,1},{3,0},{4,7},{5,6},{6,5},{7,4},{8,11},{9,10},{10,... | collective-permute-start | bytes 196616 | tf_op jit(solution)/shard_map/ppermute | solution.py:22
  109.5 5.0 %collective-permute-start.24 = (f32[128,128]{1,0:T(8,128)S(1)}, f32[128,128]{1,0:T(8,128)S(1)}, u32[]{:S(2)}, u32[]{:S(2)}) collective-permute-start(f32[128,128]{1,0:T(8,128)S(1)} %get-tuple-element.32), channel_id=1, source_target_pairs={{0,2},{1,3},{2,0},{3,1},{4,6},{5,7},{6,4},{7,5},{8,10},{9,11},{10,... | collective-permute-start | bytes 196616 | tf_op jit(solution)/shard_map/ppermute | solution.py:22
  110.2 4.3 %collective-permute-start.23 = (f32[128,128]{1,0:T(8,128)S(1)}, f32[128,128]{1,0:T(8,128)S(1)}, u32[]{:S(2)}, u32[]{:S(2)}) collective-permute-start(f32[128,128]{1,0:T(8,128)S(1)} %get-tuple-element.32), channel_id=1, source_target_pairs={{0,1},{1,0},{2,3},{3,2},{4,5},{5,4},{6,7},{7,6},{8,9},{9,8},{10,11... | collective-permute-start | bytes 196616 | tf_op jit(solution)/shard_map/ppermute | solution.py:22
where the time goes:
time: 115 us
  Pallas kernels  68 us (59%)
  starting transfers between devices  22.4 us (19%)
  waiting for transfers between devices  19.7 us (17%)
  local copies, waits for them, and re-layouts  3.51 us (3%)
    pallas_call x2, Pallas kernels, on_device(): call(functools.partial(next_body, workers_n), [wide, tall], workers_n + 6...  41.9 us
    ppermute x26, starting transfers between devices, swap(): return lax.ppermute(value, axis, [(i, i ^ mask) for i in range(size)])  22.4 us
    pallas_call x1, Pallas kernels, on_device(): call(functools.partial(first_body, jobs_n, workers_n), [wide, tall, ((col...  20.5 us
    ppermute x26, waiting for transfers between devices, swap(): return lax.ppermute(value, axis, [(i, i ^ mask) for i in range(size)])  19.7 us
    pallas_call x1, Pallas kernels, on_device(): call(functools.partial(moment_body, workers_n), [((feat, feat), F32), ((1...  5.34 us
    unnamed x14, local copies, waits for them, and re-layouts  2.91 us
  transfers between devices with their start and end apart: 26, of which 12 were waited for; matrix products, arithmetic and copies ran while one was open for 1% of the time, Pallas kernels for 0%

commit v1 on v0

--- a/solution.py
+++ b/solution.py
@@ -10,7 +10,7 @@
 
 SWEEPS = 3
 LANES = 128
-TILE = 512
+TILE = 1024
 CHUNK = 1024
 BY_ROW = (((1,), (1,)), ((), ()))
 BY_COLUMN = (((0,), (0,)), ((), ()))
@@ -38,22 +38,36 @@
     return col + log_total - both[:, :cols], log_total
 
 
-def scores_of(proj_ref, jobs_ref, at):
-    return lax.dot_general(
-        proj_ref[...], jobs_ref[pl.ds(at, TILE), :], BY_ROW, preferred_element_type=F32
-    )
+def scores_of(rows_ref, jobs_ref, at):
+    jobs = jobs_ref[pl.ds(at, TILE), :]
+    if rows_ref.shape[1] > jobs.shape[1]:
+        jobs = jnp.concatenate([jobs, jnp.ones_like(jobs)], axis=1)
+    return lax.dot_general(rows_ref[...], jobs, BY_ROW, preferred_element_type=F32)
+
+
+def with_shift(rows_ref, proj_ref, shift):
+    feat = proj_ref.shape[1]
+    lane = lax.broadcasted_iota(jnp.int32, shift.shape, 1)
+    parts = jnp.zeros_like(shift)
+    for k in range(3):
+        part = shift.astype(BF16).astype(F32)
+        parts = jnp.where(lane == k, part, parts)
+        shift = shift - part
+    rows_ref[:, :feat] = proj_ref[...]
+    rows_ref[:, feat:] = parts.astype(BF16)
 
 
 def sweep_rows_and_columns(proj_ref, jobs_ref, v_ref, shift_ref, mass_ref, out_ref, fresh_ref, scratch):
-    e_ref, sum_ref, gain_ref = scratch
+    e_ref, sum_ref, gain_ref, *shifted = scratch
     rows, cols = proj_ref.shape[0], jobs_ref.shape[0]
+    rows_ref = proj_ref
+    if shift_ref is not None:
+        (rows_ref,) = shifted
+        with_shift(rows_ref, proj_ref, shift_ref[...])
 
     def fast(k, carry):
         at = pl.multiple_of(k * TILE, TILE)
-        z = scores_of(proj_ref, jobs_ref, at) + v_ref[:, pl.ds(at, TILE)]
-        if shift_ref is not None:
-            z = z + widen(shift_ref[...], TILE)
-        e = jnp.exp(z)
+        e = jnp.exp(scores_of(rows_ref, jobs_ref, at) + v_ref[:, pl.ds(at, TILE)])
         e_ref[:, pl.ds(at, TILE)] = e
         part = e[:, :LANES]
         for j in range(1, TILE // LANES):
@@ -155,18 +169,19 @@
 
 
 def first_body(jobs_n, workers_n, *refs):
-    job_pieces, refs = refs[: 3 * jobs_n], refs[3 * jobs_n :]
+    job_pieces, refs = refs[:8], refs[8:]
     messages, refs = refs[:jobs_n], refs[jobs_n:]
     affinity_ref, mass_ref, log_total_ref, *refs = refs
     out_ref, fresh_ref, jobs_ref, workers_ref, proj_ref, col_ref, *refs = refs
     start_ref, *scratch = refs
     job, worker = lax.axis_index("job"), lax.axis_index("worker")
     size = job_pieces[0].shape[0]
-    for s in range(jobs_n):
-        own, across, other = job_pieces[3 * s : 3 * s + 3]
-        for mask, piece in ((0, own[...]), (2, across[...]), (1, other[:size, :]), (3, other[size:, :])):
+    for mask in range(4):
+        own, others = job_pieces[mask], job_pieces[4 + mask]
+        for s in range(jobs_n):
+            block = own[...] if s == 0 else others[(s - 1) * size : s * size, :]
             at = pl.multiple_of((s * workers_n + (worker ^ mask)) * size, size)
-            jobs_ref[pl.ds(at, size), :] = piece
+            jobs_ref[pl.ds(at, size), :] = block
     size = workers_ref.shape[0] // jobs_n
     high = (messages[0].shape[0] - size) // 3
     block = jobs_ref.shape[0] // jobs_n
@@ -204,18 +219,19 @@
 def moment_body(workers_n, *refs):
     piece_refs, refs = refs[:workers_n], refs[workers_n:]
     proj_ref, jobs_ref, workers_ref, col_ref, shift_ref, *refs = refs
-    moment_ref, u_ref, v_ref, weighted_ref = refs
+    moment_ref, u_ref, v_ref, weighted_ref, rows_ref = refs
     rows, cols = proj_ref.shape[0], jobs_ref.shape[0]
     v, log_total = new_v(col_ref[...], [ref[...] for ref in piece_refs])
     v_ref[...] = v
     weighted_ref[...] = jnp.zeros_like(weighted_ref)
+    u = shift_ref[...] - log_total
+    with_shift(rows_ref, proj_ref, u)
 
     def add(k, carry):
         at = pl.multiple_of(k * TILE, TILE)
-        z = scores_of(proj_ref, jobs_ref, at) + widen(shift_ref[...] - log_total, TILE)
-        coupling = jnp.exp(z + v_ref[:, pl.ds(at, TILE)]).astype(BF16)
+        z = scores_of(rows_ref, jobs_ref, at) + v_ref[:, pl.ds(at, TILE)]
         weighted_ref[...] = weighted_ref[...] + jnp.dot(
-            coupling, jobs_ref[pl.ds(at, TILE), :], preferred_element_type=F32
+            jnp.exp(z).astype(BF16), jobs_ref[pl.ds(at, TILE), :], preferred_element_type=F32
         )
         return carry
 
@@ -233,21 +249,21 @@
     )
     wide = high.shape[1]
     moment_ref[...] = parts[:, :wide] + (parts[:, wide : 2 * wide] + parts[:, 2 * wide :])
-    u = shift_ref[...] - log_total
     diagonal = diagonal_mask()
     for k in range(rows // LANES):
         block = jnp.where(diagonal, u[k * LANES : (k + 1) * LANES, :], 0.0)
         u_ref[:, k * LANES : (k + 1) * LANES] = jnp.sum(block, axis=0, keepdims=True)
 
 
-def call(body, outs, n_in, scratch):
+def call(body, outs, n_in, scratch, rows_shape=None):
     vmem = pl.BlockSpec(memory_space=pltpu.VMEM)
     return pl.pallas_call(
         body,
         out_shape=tuple(jax.ShapeDtypeStruct(shape, dtype) for shape, dtype in outs),
         in_specs=[vmem] * n_in,
         out_specs=(vmem,) * len(outs),
-        scratch_shapes=[pltpu.VMEM(shape, F32) for shape in scratch],
+        scratch_shapes=[pltpu.VMEM(shape, F32) for shape in scratch]
+        + ([pltpu.VMEM(rows_shape, BF16)] if rows_shape else []),
         compiler_params=pltpu.CompilerParams(vmem_limit_bytes=40 << 20),
     )
 
@@ -289,11 +305,11 @@
             worker_mass.reshape(-1, LANES),
         )
         job_pieces = []
-        for own in over_job(job_feat):
-            across = swap(own, "worker", workers_n, 2)
-            both = jnp.concatenate([own, across], axis=0)
-            other = swap(both, "worker", workers_n, 1)
-            job_pieces += [own, across, other]
+        own, *others = over_job(job_feat)
+        for held in (own, jnp.concatenate(others, axis=0)):
+            across = swap(held, "worker", workers_n, 2)
+            job_pieces += [held, swap(held, "worker", workers_n, 1)]
+            job_pieces += [across, swap(across, "worker", workers_n, 1)]
         messages = over_job(message)
         work = [(rows, cols), (rows, LANES), (rows, LANES)]
         out, shift, jobs, workers, proj, log_job = call(
@@ -306,7 +322,7 @@
                 ((rows, feat), BF16),
                 ((1, cols), F32),
             ],
-            4 * jobs_n + 3,
+            jobs_n + 11,
             [(1, cols)] + work,
         )(*job_pieces, *messages, affinity, mass, log_total)
         for _ in range(1, SWEEPS):
@@ -315,12 +331,14 @@
                 [wide, tall],
                 workers_n + 6,
                 [(1, cols)] + work,
+                (rows, 2 * feat),
             )(*over_worker(out), proj, jobs, log_job, shift, mass, log_total)
         moment, pot_u, pot_v = call(
             functools.partial(moment_body, workers_n),
             [((feat, feat), F32), ((1, rows), F32), ((1, cols), F32)],
             workers_n + 5,
             [(rows, feat)],
+            (rows, 2 * feat),
         )(*over_worker(out), proj, jobs, workers, log_job, shift)
         moment = sum(over_worker(moment))
         own_jobs = cols // jobs_n

time: 115 us -> 106 us (0.922)
  Pallas kernels: 68 us -> 57.3 us
  waiting for transfers between devices: 19.7 us -> 25.9 us
  local copies, waits for them, and re-layouts: 3.51 us -> 0.66 us
  starting transfers between devices: 22.4 us -> 20.9 us
    pallas_call x2, Pallas kernels: 41.9 us -> 34 us  [on_device(): call(functools.partial(next_body, workers_n), [wide, tall], workers_n + 6...]
    ppermute x26 -> x24, waiting for transfers between devices: 19.7 us -> 25.9 us  [swap(): return lax.ppermute(value, axis, [(i, i ^ mask) for i in range(size)])]
    pallas_call x1, Pallas kernels: 20.5 us -> 17.6 us  [on_device(): call(functools.partial(first_body, jobs_n, workers_n), [wide, tall, ((col...]
    unnamed x14 -> x16, local copies, waits for them, and re-layouts: 2.91 us -> 0.05 us
    ppermute x26 -> x24, starting transfers between devices: 22.4 us -> 20.9 us  [swap(): return lax.ppermute(value, axis, [(i, i ^ mask) for i in range(size)])]
  transfers between devices with their start and end apart: 26 -> 24, of which waited for: 12 -> 15; matrix products, arithmetic and copies ran while one was open for 1% -> 1% of each run, Pallas kernels for 0% -> 0%
where the time goes in v1:
time: 106 us
  Pallas kernels  57.3 us (54%)
  waiting for transfers between devices  25.9 us (24%)
  starting transfers between devices  20.9 us (20%)
    pallas_call x2, Pallas kernels, on_device(): call(functools.partial(next_body, workers_n), [wide, tall], workers_n + 6...  34 us
    ppermute x24, waiting for transfers between devices, swap(): return lax.ppermute(value, axis, [(i, i ^ mask) for i in range(size)])  25.9 us
    ppermute x24, starting transfers between devices, swap(): return lax.ppermute(value, axis, [(i, i ^ mask) for i in range(size)])  20.9 us
    pallas_call x1, Pallas kernels, on_device(): call(functools.partial(first_body, jobs_n, workers_n), [wide, tall, ((col...  17.6 us
    pallas_call x1, Pallas kernels, on_device(): call(functools.partial(moment_body, workers_n), [((feat, feat), F32), ((1...  5.33 us
  transfers between devices with their start and end apart: 24, of which 15 were waited for; matrix products, arithmetic and copies ran while one was open for 1% of the time, Pallas kernels for 0%

profile of v1, /device:TPU:0, one launch (start us, length us, event | category | flops | bytes accessed | tf_op | source)
XLA Modules:
  0.0 106.1 jit_solution(14799561122490657366)
XLA Ops:
  0.6 3.1 %collective-permute-start.3 = (bf16[256,128]{1,0:T(8,128)(2,1)}, bf16[256,128]{1,0:T(8,128)(2,1)S(1)}, u32[]{:S(2)}, u32[]{:S(2)}) collective-permute-start(bf16[256,128]{1,0:T(8,128)(2,1)} %refs_0_.1), channel_id=1, source_target_pairs={{0,4},{4,0},{8,12},{12,8},{1,5},{5,1},{9,13},{13,9},{2,6},{6,2},{1... | collective-permute-start | bytes 196616 | tf_op jit(solution)/shard_map/ppermute | solution.py:22
  3.7 2.6 %collective-permute-start.4 = (bf16[256,128]{1,0:T(8,128)(2,1)}, bf16[256,128]{1,0:T(8,128)(2,1)S(1)}, u32[]{:S(2)}, u32[]{:S(2)}) collective-permute-start(bf16[256,128]{1,0:T(8,128)(2,1)} %refs_0_.1), channel_id=1, source_target_pairs={{0,8},{4,12},{8,0},{12,4},{1,9},{5,13},{9,1},{13,5},{2,10},{6,14},... | collective-permute-start | bytes 196616 | tf_op jit(solution)/shard_map/ppermute | solution.py:22
  6.4 4.9 %collective-permute-done.4 = bf16[256,128]{1,0:T(8,128)(2,1)S(1)} collective-permute-done((bf16[256,128]{1,0:T(8,128)(2,1)}, bf16[256,128]{1,0:T(8,128)(2,1)S(1)}, u32[]{:S(2)}, u32[]{:S(2)}) %collective-permute-start.4) | collective-permute-done | bytes 65568 | tf_op jit(solution)/shard_map/ppermute | solution.py:22
  11.3 0.0 copy-start
  11.3 0.0 copy-start.1
  11.3 1.4 %collective-permute-done.5 = bf16[256,128]{1,0:T(8,128)(2,1)S(1)} collective-permute-done((bf16[256,128]{1,0:T(8,128)(2,1)}, bf16[256,128]{1,0:T(8,128)(2,1)S(1)}, u32[]{:S(2)}, u32[]{:S(2)}) %collective-permute-start.5) | collective-permute-done | bytes 65568 | tf_op jit(solution)/shard_map/ppermute | solution.py:22
  12.7 0.0 copy-start.3
  12.7 1.6 %collective-permute-start.7 = (bf16[768,128]{1,0:T(8,128)(2,1)S(1)}, bf16[768,128]{1,0:T(8,128)(2,1)S(1)}, u32[]{:S(2)}, u32[]{:S(2)}) collective-permute-start(bf16[768,128]{1,0:T(8,128)(2,1)S(1)} %constant_dynamic-update-slice_fusion.refs_4_), channel_id=1, source_target_pairs={{0,2},{1,3},{2,0},{3,1},{4,6},{5,7},{6,4},{7,5},{8,10},{9,11},{10,... | collective-permute-start | bytes 589832 | tf_op jit(solution)/shard_map/ppermute | solution.py:22
  14.2 4.2 %collective-permute-done.7.refs_6_ = bf16[768,128]{1,0:T(8,128)(2,1)S(1)} collective-permute-done((bf16[768,128]{1,0:T(8,128)(2,1)S(1)}, bf16[768,128]{1,0:T(8,128)(2,1)S(1)}, u32[]{:S(2)}, u32[]{:S(2)}) %collective-permute-start.7) | collective-permute-done | bytes 196640 | tf_op jit(solution)/shard_map/ppermute | solution.py:22
  18.4 0.0 collective-permute-start.8
  18.4 1.5 %collective-permute-start.1 = (bf16[256,128]{1,0:T(8,128)(2,1)S(1)}, bf16[256,128]{1,0:T(8,128)(2,1)S(1)}, u32[]{:S(2)}, u32[]{:S(2)}) collective-permute-start(bf16[256,128]{1,0:T(8,128)(2,1)S(1)} %copy-done), channel_id=1, source_target_pairs={{0,2},{1,3},{2,0},{3,1},{4,6},{5,7},{6,4},{7,5},{8,10},{9,11},{10,... | collective-permute-start | bytes 196616 | tf_op jit(solution)/shard_map/ppermute | solution.py:22
  19.9 0.2 collective-permute-start
  20.1 0.0 copy-start.2
  20.2 0.4 pack.1
  20.5 1.9 %collective-permute-start.11 = (bf16[304,128]{1,0:T(8,128)(2,1)S(1)}, bf16[304,128]{1,0:T(8,128)(2,1)S(1)}, u32[]{:S(2)}, u32[]{:S(2)}) collective-permute-start(bf16[304,128]{1,0:T(8,128)(2,1)S(1)} %get-tuple-element.19.refs_8_), channel_id=1, source_target_pairs={{0,12},{4,8},{8,4},{12,0},{1,13},{5,9},{9,5},{13,1},{2,14},{6,10},... | collective-permute-start | bytes 233480 | tf_op jit(solution)/shard_map/ppermute | solution.py:22
  22.4 0.5 collective-permute-done.1.refs_2_
  22.9 1.6 %collective-permute-start.10 = (bf16[304,128]{1,0:T(8,128)(2,1)S(1)}, bf16[304,128]{1,0:T(8,128)(2,1)S(1)}, u32[]{:S(2)}, u32[]{:S(2)}) collective-permute-start(bf16[304,128]{1,0:T(8,128)(2,1)S(1)} %get-tuple-element.19.refs_8_), channel_id=1, source_target_pairs={{0,8},{4,12},{8,0},{12,4},{1,9},{5,13},{9,1},{13,5},{2,10},{6,14},... | collective-permute-start | bytes 233480 | tf_op jit(solution)/shard_map/ppermute | solution.py:22
  24.5 0.0 collective-permute-done.refs_1_
  24.5 0.8 collective-permute-start.9
  25.3 2.4 %collective-permute-done.11.refs_11_ = bf16[304,128]{1,0:T(8,128)(2,1)S(1)} collective-permute-done((bf16[304,128]{1,0:T(8,128)(2,1)S(1)}, bf16[304,128]{1,0:T(8,128)(2,1)S(1)}, u32[]{:S(2)}, u32[]{:S(2)}) %collective-permute-start.11) | collective-permute-done | bytes 77856 | tf_op jit(solution)/shard_map/ppermute | solution.py:22
  27.7 2.5 %collective-permute-done.10.refs_10_ = bf16[304,128]{1,0:T(8,128)(2,1)S(1)} collective-permute-done((bf16[304,128]{1,0:T(8,128)(2,1)S(1)}, bf16[304,128]{1,0:T(8,128)(2,1)S(1)}, u32[]{:S(2)}, u32[]{:S(2)}) %collective-permute-start.10) | collective-permute-done | bytes 77856 | tf_op jit(solution)/shard_map/ppermute | solution.py:22
  30.3 0.2 collective-permute-done.9.refs_9_
  30.5 17.6 %shard_map.94 = (f32[1,4224]{1,0:T(1,128)S(1)}, f32[1024,128]{1,0:T(8,128)S(1)}, bf16[4096,128]{1,0:T(8,128)(2,1)S(1)}, bf16[1024,128]{1,0:T(8,128)(2,1)S(1)}, b...) custom-call(bf16[256,128]{1,0:T(8,128)(2,1)S(1)} %copy-done, bf16[256,128]{1,0:T(8,128)(2,1)S(1)} %collective-permute-done.refs_1_, ...), custom_call_target="tpu_custom_call" | custom-call | tf_op jit(solution)/shard_map/pallas_call | solution.py:315
  48.1 0.1 collective-permute-start.14
  48.1 1.5 %collective-permute-start.13 = (f32[1,4224]{1,0:T(1,128)S(1)}, f32[1,4224]{1,0:T(1,128)S(1)}, u32[]{:S(2)}, u32[]{:S(2)}) collective-permute-start(f32[1,4224]{1,0:T(1,128)S(1)} %get-tuple-element.22.refs_0_), channel_id=1, source_target_pairs={{0,2},{1,3},{2,0},{3,1},{4,6},{5,7},{6,4},{7,5},{8,10},{9,11},{10,... | collective-permute-start | bytes 50696 | tf_op jit(solution)/shard_map/ppermute | solution.py:22
  49.6 0.4 collective-permute-start.12
  50.0 1.5 %collective-permute-done.14.refs_3_ = f32[1,4224]{1,0:T(1,128)S(1)} collective-permute-done((f32[1,4224]{1,0:T(1,128)S(1)}, f32[1,4224]{1,0:T(1,128)S(1)}, u32[]{:S(2)}, u32[]{:S(2)}) %collective-permute-start.14) | collective-permute-done | bytes 16928 | tf_op jit(solution)/shard_map/ppermute | solution.py:22
  51.4 0.5 collective-permute-done.13.refs_2_
  52.0 16.9 %shard_map.95 = (f32[1,4224]{1,0:T(1,128)S(1)}, f32[1024,128]{1,0:T(8,128)S(1)}) custom-call(f32[1,4224]{1,0:T(1,128)S(1)} %get-tuple-element.22.refs_0_, f32[1,4224]{1,0:T(1,128)S(1)} %collective-permute-done.12.refs_1_, f32[1,4224]{1,0:T(1,128)S(1)} %collective-permute-done.13.refs_2_, f32[1,4224]{1,0:T(1,128)S(1)} %collective-permute-done.14.refs_3_, ...), custom_call_target="tpu_custom_call" | custom-call | tf_op jit(solution)/shard_map/pallas_call | solution.py:329
  68.8 0.6 collective-permute-start.17
  69.4 1.2 %collective-permute-start.16 = (f32[1,4224]{1,0:T(1,128)S(1)}, f32[1,4224]{1,0:T(1,128)S(1)}, u32[]{:S(2)}, u32[]{:S(2)}) collective-permute-start(f32[1,4224]{1,0:T(1,128)S(1)} %get-tuple-element.27.refs_0_), channel_id=1, source_target_pairs={{0,2},{1,3},{2,0},{3,1},{4,6},{5,7},{6,4},{7,5},{8,10},{9,11},{10,... | collective-permute-start | bytes 50696 | tf_op jit(solution)/shard_map/ppermute | solution.py:22
  70.7 0.1 collective-permute-start.15
  70.8 1.3 %collective-permute-done.17.refs_3_ = f32[1,4224]{1,0:T(1,128)S(1)} collective-permute-done((f32[1,4224]{1,0:T(1,128)S(1)}, f32[1,4224]{1,0:T(1,128)S(1)}, u32[]{:S(2)}, u32[]{:S(2)}) %collective-permute-start.17) | collective-permute-done | bytes 16928 | tf_op jit(solution)/shard_map/ppermute | solution.py:22
  72.1 1.2 %collective-permute-done.16.refs_2_ = f32[1,4224]{1,0:T(1,128)S(1)} collective-permute-done((f32[1,4224]{1,0:T(1,128)S(1)}, f32[1,4224]{1,0:T(1,128)S(1)}, u32[]{:S(2)}, u32[]{:S(2)}) %collective-permute-start.16) | collective-permute-done | bytes 16928 | tf_op jit(solution)/shard_map/ppermute | solution.py:22
  73.3 17.1 %shard_map.96 = (f32[1,4224]{1,0:T(1,128)S(1)}, f32[1024,128]{1,0:T(8,128)S(1)}) custom-call(f32[1,4224]{1,0:T(1,128)S(1)} %get-tuple-element.27.refs_0_, f32[1,4224]{1,0:T(1,128)S(1)} %collective-permute-done.15.refs_1_, f32[1,4224]{1,0:T(1,128)S(1)} %collective-permute-done.16.refs_2_, f32[1,4224]{1,0:T(1,128)S(1)} %collective-permute-done.17.refs_3_, ...), custom_call_target="tpu_custom_call" | custom-call | tf_op jit(solution)/shard_map/pallas_call | solution.py:329
  90.4 0.1 collective-permute-start.20
  90.5 1.8 %collective-permute-start.19 = (f32[1,4224]{1,0:T(1,128)S(1)}, f32[1,4224]{1,0:T(1,128)S(1)}, u32[]{:S(2)}, u32[]{:S(2)}) collective-permute-start(f32[1,4224]{1,0:T(1,128)S(1)} %get-tuple-element.29.refs_0_), channel_id=1, source_target_pairs={{0,2},{1,3},{2,0},{3,1},{4,6},{5,7},{6,4},{7,5},{8,10},{9,11},{10,... | collective-permute-start | bytes 50696 | tf_op jit(solution)/shard_map/ppermute | solution.py:22
  92.3 0.1 collective-permute-start.18
  92.4 1.3 %collective-permute-done.20.refs_3_ = f32[1,4224]{1,0:T(1,128)S(1)} collective-permute-done((f32[1,4224]{1,0:T(1,128)S(1)}, f32[1,4224]{1,0:T(1,128)S(1)}, u32[]{:S(2)}, u32[]{:S(2)}) %collective-permute-start.20) | collective-permute-done | bytes 16928 | tf_op jit(solution)/shard_map/ppermute | solution.py:22
  93.7 0.7 collective-permute-done.19.refs_2_
  94.3 5.3 %shard_map.97 = (f32[128,128]{1,0:T(8,128)S(1)}, f32[1,1024]{1,0:T(1,128)}, f32[1,4096]{1,0:T(1,128)S(1)}) custom-call(f32[1,4224]{1,0:T(1,128)S(1)} %get-tuple-element.29.refs_0_, f32[1,4224]{1,0:T(1,128)S(1)} %collective-permute-done.18.refs_1_, f32[1,4224]{1,0:T(1,128)S(1)} %collective-permute-done.19.refs_2_, ...), custom_call_target="tpu_custom_call" | custom-call | tf_op jit(solution)/shard_map/pallas_call | solution.py:336
  99.7 0.5 collective-permute-start.23
  100.2 1.2 %collective-permute-start.22 = (f32[128,128]{1,0:T(8,128)S(1)}, f32[128,128]{1,0:T(8,128)S(1)}, u32[]{:S(2)}, u32[]{:S(2)}) collective-permute-start(f32[128,128]{1,0:T(8,128)S(1)} %get-tuple-element.32), channel_id=1, source_target_pairs={{0,2},{1,3},{2,0},{3,1},{4,6},{5,7},{6,4},{7,5},{8,10},{9,11},{10,... | collective-permute-start | bytes 196616 | tf_op jit(solution)/shard_map/ppermute | solution.py:22
  101.4 0.1 collective-permute-start.21
  101.5 0.6 slice.3
  102.1 1.6 %collective-permute-done.23 = f32[128,128]{1,0:T(8,128)S(1)} collective-permute-done((f32[128,128]{1,0:T(8,128)S(1)}, f32[128,128]{1,0:T(8,128)S(1)}, u32[]{:S(2)}, u32[]{:S(2)}) %collective-permute-start.23) | collective-permute-done | bytes 65568 | tf_op jit(solution)/shard_map/ppermute | solution.py:22
  103.8 1.7 %collective-permute-done.22 = f32[128,128]{1,0:T(8,128)S(1)} collective-permute-done((f32[128,128]{1,0:T(8,128)S(1)}, f32[128,128]{1,0:T(8,128)S(1)}, u32[]{:S(2)}, u32[]{:S(2)}) %collective-permute-start.22) | collective-permute-done | bytes 65568 | tf_op jit(solution)/shard_map/ppermute | solution.py:22
  105.5 0.7 add_subtract_fusion
  (24 shorter events, 0.1 us)
Async XLA Ops:
  0.6 5.7 %collective-permute-start.3 = (bf16[256,128]{1,0:T(8,128)(2,1)}, bf16[256,128]{1,0:T(8,128)(2,1)S(1)}, u32[]{:S(2)}, u32[]{:S(2)}) collective-permute-start(bf16[256,128]{1,0:T(8,128)(2,1)} %refs_0_.1), channel_id=1, source_target_pairs={{0,4},{4,0},{8,12},{12,8},{1,5},{5,1},{9,13},{13,9},{2,6},{6,2},{1... | collective-permute-start | bytes 196616 | tf_op jit(solution)/shard_map/ppermute | solution.py:22
  3.7 7.5 %collective-permute-start.4 = (bf16[256,128]{1,0:T(8,128)(2,1)}, bf16[256,128]{1,0:T(8,128)(2,1)S(1)}, u32[]{:S(2)}, u32[]{:S(2)}) collective-permute-start(bf16[256,128]{1,0:T(8,128)(2,1)} %refs_0_.1), channel_id=1, source_target_pairs={{0,8},{4,12},{8,0},{12,4},{1,9},{5,13},{9,1},{13,5},{2,10},{6,14},... | collective-permute-start | bytes 196616 | tf_op jit(solution)/shard_map/ppermute | solution.py:22
  6.3 6.3 %collective-permute-start.5 = (bf16[256,128]{1,0:T(8,128)(2,1)}, bf16[256,128]{1,0:T(8,128)(2,1)S(1)}, u32[]{:S(2)}, u32[]{:S(2)}) collective-permute-start(bf16[256,128]{1,0:T(8,128)(2,1)} %refs_0_.1), channel_id=1, source_target_pairs={{0,12},{4,8},{8,4},{12,0},{1,13},{5,9},{9,5},{13,1},{2,14},{6,10},... | collective-permute-start | bytes 196616 | tf_op jit(solution)/shard_map/ppermute | solution.py:22
  11.2 8.9 %copy-start.4 = (f32[1024]{0:T(1024)S(1)}, f32[1024]{0:T(1024)}, u32[]{:S(2)}) copy-start(f32[1024]{0:T(1024)} %param.11) | copy-start | bytes 12292
  11.2 8.9 %copy-start.5 = (f32[1024]{0:T(1024)S(1)}, f32[1024]{0:T(1024)}, u32[]{:S(2)}) copy-start(f32[1024]{0:T(1024)} %param.10) | copy-start | bytes 12292
  11.3 7.2 %copy-start = (bf16[256,128]{1,0:T(8,128)(2,1)S(1)}, bf16[256,128]{1,0:T(8,128)(2,1)}, u32[]{:S(2)}) copy-start(bf16[256,128]{1,0:T(8,128)(2,1)} %refs_0_.1) | copy-start | bytes 196612
  11.3 8.9 %copy-start.1 = (bf16[256,128]{1,0:T(8,128)(2,1)S(1)}, bf16[256,128]{1,0:T(8,128)(2,1)}, u32[]{:S(2)}) copy-start(bf16[256,128]{1,0:T(8,128)(2,1)} %workers_hbm.1) | copy-start | bytes 196612
  12.7 7.5 %copy-start.3 = (f32[1024]{0:T(1024)S(1)}, f32[1024]{0:T(1024)}, u32[]{:S(2)}) copy-start(f32[1024]{0:T(1024)} %param.12) | copy-start | bytes 12292
  12.7 5.7 %collective-permute-start.7 = (bf16[768,128]{1,0:T(8,128)(2,1)S(1)}, bf16[768,128]{1,0:T(8,128)(2,1)S(1)}, u32[]{:S(2)}, u32[]{:S(2)}) collective-permute-start(bf16[768,128]{1,0:T(8,128)(2,1)S(1)} %constant_dynamic-update-slice_fusion.refs_4_), channel_id=1, source_target_pairs={{0,2},{1,3},{2,0},{3,1},{4,6},{5,7},{6,4},{7,5},{8,10},{9,11},{10,... | collective-permute-start | bytes 589832 | tf_op jit(solution)/shard_map/ppermute | solution.py:22
  14.2 16.2 %collective-permute-start.6 = (bf16[768,128]{1,0:T(8,128)(2,1)S(1)}, bf16[768,128]{1,0:T(8,128)(2,1)S(1)}, u32[]{:S(2)}, u32[]{:S(2)}) collective-permute-start(bf16[768,128]{1,0:T(8,128)(2,1)S(1)} %constant_dynamic-update-slice_fusion.refs_4_), channel_id=1, source_target_pairs={{0,1},{1,0},{2,3},{3,2},{4,5},{5,4},{6,7},{7,6},{8,9},{9,8},{10,11... | collective-permute-start | bytes 589832 | tf_op jit(solution)/shard_map/ppermute | solution.py:22
  18.4 12.0 %collective-permute-start.8 = (bf16[768,128]{1,0:T(8,128)(2,1)S(1)}, bf16[768,128]{1,0:T(8,128)(2,1)S(1)}, u32[]{:S(2)}, u32[]{:S(2)}) collective-permute-start(bf16[768,128]{1,0:T(8,128)(2,1)S(1)} %collective-permute-done.7.refs_6_), channel_id=1, source_target_pairs={{0,1},{1,0},{2,3},{3,2},{4,5},{5,4},{6,7},{7,6},{8,9},{9,8},{10,11... | collective-permute-start | bytes 589832 | tf_op jit(solution)/shard_map/ppermute | solution.py:22
  18.4 4.5 %collective-permute-start.1 = (bf16[256,128]{1,0:T(8,128)(2,1)S(1)}, bf16[256,128]{1,0:T(8,128)(2,1)S(1)}, u32[]{:S(2)}, u32[]{:S(2)}) collective-permute-start(bf16[256,128]{1,0:T(8,128)(2,1)S(1)} %copy-done), channel_id=1, source_target_pairs={{0,2},{1,3},{2,0},{3,1},{4,6},{5,7},{6,4},{7,5},{8,10},{9,11},{10,... | collective-permute-start | bytes 196616 | tf_op jit(solution)/shard_map/ppermute | solution.py:22
  19.9 4.6 %collective-permute-start = (bf16[256,128]{1,0:T(8,128)(2,1)S(1)}, bf16[256,128]{1,0:T(8,128)(2,1)S(1)}, u32[]{:S(2)}, u32[]{:S(2)}) collective-permute-start(bf16[256,128]{1,0:T(8,128)(2,1)S(1)} %copy-done), channel_id=1, source_target_pairs={{0,1},{1,0},{2,3},{3,2},{4,5},{5,4},{6,7},{7,6},{8,9},{9,8},{10,11... | collective-permute-start | bytes 196616 | tf_op jit(solution)/shard_map/ppermute | solution.py:22
  20.1 10.3 %copy-start.2 = (bf16[128,128]{1,0:T(8,128)(2,1)S(1)}, bf16[128,128]{1,0:T(8,128)(2,1)}, u32[]{:S(2)}) copy-start(bf16[128,128]{1,0:T(8,128)(2,1)} %refs_12_.1) | copy-start | bytes 98308
  20.5 7.2 %collective-permute-start.11 = (bf16[304,128]{1,0:T(8,128)(2,1)S(1)}, bf16[304,128]{1,0:T(8,128)(2,1)S(1)}, u32[]{:S(2)}, u32[]{:S(2)}) collective-permute-start(bf16[304,128]{1,0:T(8,128)(2,1)S(1)} %get-tuple-element.19.refs_8_), channel_id=1, source_target_pairs={{0,12},{4,8},{8,4},{12,0},{1,13},{5,9},{9,5},{13,1},{2,14},{6,10},... | collective-permute-start | bytes 233480 | tf_op jit(solution)/shard_map/ppermute | solution.py:22
  22.9 7.4 %collective-permute-start.10 = (bf16[304,128]{1,0:T(8,128)(2,1)S(1)}, bf16[304,128]{1,0:T(8,128)(2,1)S(1)}, u32[]{:S(2)}, u32[]{:S(2)}) collective-permute-start(bf16[304,128]{1,0:T(8,128)(2,1)S(1)} %get-tuple-element.19.refs_8_), channel_id=1, source_target_pairs={{0,8},{4,12},{8,0},{12,4},{1,9},{5,13},{9,1},{13,5},{2,10},{6,14},... | collective-permute-start | bytes 233480 | tf_op jit(solution)/shard_map/ppermute | solution.py:22
  24.5 6.0 %collective-permute-start.9 = (bf16[304,128]{1,0:T(8,128)(2,1)S(1)}, bf16[304,128]{1,0:T(8,128)(2,1)S(1)}, u32[]{:S(2)}, u32[]{:S(2)}) collective-permute-start(bf16[304,128]{1,0:T(8,128)(2,1)S(1)} %get-tuple-element.19.refs_8_), channel_id=1, source_target_pairs={{0,4},{4,0},{8,12},{12,8},{1,5},{5,1},{9,13},{13,9},{2,6},{6,2},{1... | collective-permute-start | bytes 233480 | tf_op jit(solution)/shard_map/ppermute | solution.py:22
  27.7 2.7 %collective-permute-start.2 = (bf16[256,128]{1,0:T(8,128)(2,1)S(1)}, bf16[256,128]{1,0:T(8,128)(2,1)S(1)}, u32[]{:S(2)}, u32[]{:S(2)}) collective-permute-start(bf16[256,128]{1,0:T(8,128)(2,1)S(1)} %collective-permute-done.1.refs_2_), channel_id=1, source_target_pairs={{0,1},{1,0},{2,3},{3,2},{4,5},{5,4},{6,7},{7,6},{8,9},{9,8},{10,11... | collective-permute-start | bytes 196616 | tf_op jit(solution)/shard_map/ppermute | solution.py:22
  48.1 3.4 %collective-permute-start.14 = (f32[1,4224]{1,0:T(1,128)S(1)}, f32[1,4224]{1,0:T(1,128)S(1)}, u32[]{:S(2)}, u32[]{:S(2)}) collective-permute-start(f32[1,4224]{1,0:T(1,128)S(1)} %get-tuple-element.22.refs_0_), channel_id=1, source_target_pairs={{0,3},{1,2},{2,1},{3,0},{4,7},{5,6},{6,5},{7,4},{8,11},{9,10},{10,... | collective-permute-start | bytes 50696 | tf_op jit(solution)/shard_map/ppermute | solution.py:22
  48.1 3.8 %collective-permute-start.13 = (f32[1,4224]{1,0:T(1,128)S(1)}, f32[1,4224]{1,0:T(1,128)S(1)}, u32[]{:S(2)}, u32[]{:S(2)}) collective-permute-start(f32[1,4224]{1,0:T(1,128)S(1)} %get-tuple-element.22.refs_0_), channel_id=1, source_target_pairs={{0,2},{1,3},{2,0},{3,1},{4,6},{5,7},{6,4},{7,5},{8,10},{9,11},{10,... | collective-permute-start | bytes 50696 | tf_op jit(solution)/shard_map/ppermute | solution.py:22
  49.6 2.4 %collective-permute-start.12 = (f32[1,4224]{1,0:T(1,128)S(1)}, f32[1,4224]{1,0:T(1,128)S(1)}, u32[]{:S(2)}, u32[]{:S(2)}) collective-permute-start(f32[1,4224]{1,0:T(1,128)S(1)} %get-tuple-element.22.refs_0_), channel_id=1, source_target_pairs={{0,1},{1,0},{2,3},{3,2},{4,5},{5,4},{6,7},{7,6},{8,9},{9,8},{10,11... | collective-permute-start | bytes 50696 | tf_op jit(solution)/shard_map/ppermute | solution.py:22
  68.8 3.2 %collective-permute-start.17 = (f32[1,4224]{1,0:T(1,128)S(1)}, f32[1,4224]{1,0:T(1,128)S(1)}, u32[]{:S(2)}, u32[]{:S(2)}) collective-permute-start(f32[1,4224]{1,0:T(1,128)S(1)} %get-tuple-element.27.refs_0_), channel_id=1, source_target_pairs={{0,3},{1,2},{2,1},{3,0},{4,7},{5,6},{6,5},{7,4},{8,11},{9,10},{10,... | collective-permute-start | bytes 50696 | tf_op jit(solution)/shard_map/ppermute | solution.py:22
  69.4 3.9 %collective-permute-start.16 = (f32[1,4224]{1,0:T(1,128)S(1)}, f32[1,4224]{1,0:T(1,128)S(1)}, u32[]{:S(2)}, u32[]{:S(2)}) collective-permute-start(f32[1,4224]{1,0:T(1,128)S(1)} %get-tuple-element.27.refs_0_), channel_id=1, source_target_pairs={{0,2},{1,3},{2,0},{3,1},{4,6},{5,7},{6,4},{7,5},{8,10},{9,11},{10,... | collective-permute-start | bytes 50696 | tf_op jit(solution)/shard_map/ppermute | solution.py:22
  70.7 2.7 %collective-permute-start.15 = (f32[1,4224]{1,0:T(1,128)S(1)}, f32[1,4224]{1,0:T(1,128)S(1)}, u32[]{:S(2)}, u32[]{:S(2)}) collective-permute-start(f32[1,4224]{1,0:T(1,128)S(1)} %get-tuple-element.27.refs_0_), channel_id=1, source_target_pairs={{0,1},{1,0},{2,3},{3,2},{4,5},{5,4},{6,7},{7,6},{8,9},{9,8},{10,11... | collective-permute-start | bytes 50696 | tf_op jit(solution)/shard_map/ppermute | solution.py:22
  90.4 3.2 %collective-permute-start.20 = (f32[1,4224]{1,0:T(1,128)S(1)}, f32[1,4224]{1,0:T(1,128)S(1)}, u32[]{:S(2)}, u32[]{:S(2)}) collective-permute-start(f32[1,4224]{1,0:T(1,128)S(1)} %get-tuple-element.29.refs_0_), channel_id=1, source_target_pairs={{0,3},{1,2},{2,1},{3,0},{4,7},{5,6},{6,5},{7,4},{8,11},{9,10},{10,... | collective-permute-start | bytes 50696 | tf_op jit(solution)/shard_map/ppermute | solution.py:22
  90.5 3.8 %collective-permute-start.19 = (f32[1,4224]{1,0:T(1,128)S(1)}, f32[1,4224]{1,0:T(1,128)S(1)}, u32[]{:S(2)}, u32[]{:S(2)}) collective-permute-start(f32[1,4224]{1,0:T(1,128)S(1)} %get-tuple-element.29.refs_0_), channel_id=1, source_target_pairs={{0,2},{1,3},{2,0},{3,1},{4,6},{5,7},{6,4},{7,5},{8,10},{9,11},{10,... | collective-permute-start | bytes 50696 | tf_op jit(solution)/shard_map/ppermute | solution.py:22
  92.3 2.1 %collective-permute-start.18 = (f32[1,4224]{1,0:T(1,128)S(1)}, f32[1,4224]{1,0:T(1,128)S(1)}, u32[]{:S(2)}, u32[]{:S(2)}) collective-permute-start(f32[1,4224]{1,0:T(1,128)S(1)} %get-tuple-element.29.refs_0_), channel_id=1, source_target_pairs={{0,1},{1,0},{2,3},{3,2},{4,5},{5,4},{6,7},{7,6},{8,9},{9,8},{10,11... | collective-permute-start | bytes 50696 | tf_op jit(solution)/shard_map/ppermute | solution.py:22
  94.3 11.1 %copy-start.6 = (f32[128,128]{1,0:T(8,128)S(1)}, f32[128,128]{1,0:T(8,128)}, u32[]{:S(2)}) copy-start(f32[128,128]{1,0:T(8,128)} %param.13) | copy-start | bytes 196612
  99.7 4.1 %collective-permute-start.23 = (f32[128,128]{1,0:T(8,128)S(1)}, f32[128,128]{1,0:T(8,128)S(1)}, u32[]{:S(2)}, u32[]{:S(2)}) collective-permute-start(f32[128,128]{1,0:T(8,128)S(1)} %get-tuple-element.32), channel_id=1, source_target_pairs={{0,3},{1,2},{2,1},{3,0},{4,7},{5,6},{6,5},{7,4},{8,11},{9,10},{10,... | collective-permute-start | bytes 196616 | tf_op jit(solution)/shard_map/ppermute | solution.py:22
  100.2 5.3 %collective-permute-start.22 = (f32[128,128]{1,0:T(8,128)S(1)}, f32[128,128]{1,0:T(8,128)S(1)}, u32[]{:S(2)}, u32[]{:S(2)}) collective-permute-start(f32[128,128]{1,0:T(8,128)S(1)} %get-tuple-element.32), channel_id=1, source_target_pairs={{0,2},{1,3},{2,0},{3,1},{4,6},{5,7},{6,4},{7,5},{8,10},{9,11},{10,... | collective-permute-start | bytes 196616 | tf_op jit(solution)/shard_map/ppermute | solution.py:22
  101.4 4.1 %collective-permute-start.21 = (f32[128,128]{1,0:T(8,128)S(1)}, f32[128,128]{1,0:T(8,128)S(1)}, u32[]{:S(2)}, u32[]{:S(2)}) collective-permute-start(f32[128,128]{1,0:T(8,128)S(1)} %get-tuple-element.32), channel_id=1, source_target_pairs={{0,1},{1,0},{2,3},{3,2},{4,5},{5,4},{6,7},{7,6},{8,9},{9,8},{10,11... | collective-permute-start | bytes 196616 | tf_op jit(solution)/shard_map/ppermute | solution.py:22

commit v2 on v1

--- a/solution.py
+++ b/solution.py
@@ -20,6 +20,15 @@
 
 def swap(value, axis, size, mask):
     return lax.ppermute(value, axis, [(i, i ^ mask) for i in range(size)])
+
+
+def thirds_of(rest):
+    thirds = []
+    for _ in range(3):
+        part = lax.reduce_precision(rest, 8, 7)
+        thirds.append(part.astype(BF16))
+        rest = rest - part
+    return thirds
 
 
 def widen(value, width):
@@ -128,60 +137,31 @@
         lax.fori_loop(0, cols // TILE, columns, 0)
 
 
-def pack_body(workers_hbm, start_hbm, job_mass_hbm, worker_mass_hbm, message_ref, mass_ref, log_total_ref, columns_ref, worker_mass_ref, arrived):
-    size, half = workers_hbm.shape[0], start_hbm.shape[0]
-    copies = [
-        pltpu.make_async_copy(source, target, arrived.at[k])
-        for k, (source, target) in enumerate(
-            (
-                (start_hbm, columns_ref.at[pl.ds(0, half), :]),
-                (job_mass_hbm, columns_ref.at[pl.ds(half, half), :]),
-                (worker_mass_hbm, worker_mass_ref),
-                (workers_hbm, message_ref.at[pl.ds(0, size), :]),
-            )
-        )
-    ]
-    for copy in copies:
-        copy.start()
-    copies[0].wait()
-    copies[1].wait()
-    rest = columns_ref[...]
-    for k in range(3):
-        part = rest.astype(BF16)
-        message_ref[size + 2 * half * k : size + 2 * half * (k + 1), :] = part
-        rest = rest - part.astype(F32)
-    copies[2].wait()
-    diagonal = diagonal_mask()
-    for k in range(worker_mass_ref.shape[0]):
-        block = jnp.where(diagonal, worker_mass_ref[k : k + 1, :], 0.0)
-        mass_ref[k * LANES : (k + 1) * LANES, :] = jnp.broadcast_to(
-            jnp.sum(block, axis=1, keepdims=True), (LANES, LANES)
-        )
-    log_total_ref[...] = jnp.broadcast_to(
-        jnp.log(jnp.sum(worker_mass_ref[...], keepdims=True)), log_total_ref.shape
-    )
-    copies[3].wait()
-
-
 def diagonal_mask():
     shape = (LANES, LANES)
     return lax.broadcasted_iota(jnp.int32, shape, 0) == lax.broadcasted_iota(jnp.int32, shape, 1)
 
 
 def first_body(jobs_n, workers_n, *refs):
-    job_pieces, refs = refs[:8], refs[8:]
+    job_pieces, refs = refs[:10], refs[10:]
+    third_refs, refs = refs[:3], refs[3:]
     messages, refs = refs[:jobs_n], refs[jobs_n:]
-    affinity_ref, mass_ref, log_total_ref, *refs = refs
-    out_ref, fresh_ref, jobs_ref, workers_ref, proj_ref, col_ref, *refs = refs
+    affinity_ref, *refs = refs
+    out_ref, fresh_ref, jobs_ref, workers_ref, proj_ref, col_ref, mass_ref, log_total_ref, *refs = refs
     start_ref, *scratch = refs
     job, worker = lax.axis_index("job"), lax.axis_index("worker")
     size = job_pieces[0].shape[0]
-    for mask in range(4):
-        own, others = job_pieces[mask], job_pieces[4 + mask]
-        for s in range(jobs_n):
-            block = own[...] if s == 0 else others[(s - 1) * size : s * size, :]
+    kept, far, core_own, core_rest, core_far, core_last = job_pieces[:3], job_pieces[3:6], *job_pieces[6:]
+    places = (
+        [(kept[0], 0), (kept[1], 0)] + [(kept[2], k) for k in range(jobs_n - 2)],
+        [(core_own, 0)] + [(core_rest, k) for k in range(jobs_n - 1)],
+        [(far[0], 0), (far[1], 0)] + [(far[2], k) for k in range(jobs_n - 2)],
+        [(core_far, 0), (core_far, 1)] + [(core_last, k) for k in range(jobs_n - 2)],
+    )
+    for mask, sources in enumerate(places):
+        for s, (source, k) in enumerate(sources):
             at = pl.multiple_of((s * workers_n + (worker ^ mask)) * size, size)
-            jobs_ref[pl.ds(at, size), :] = block
+            jobs_ref[pl.ds(at, size), :] = source[k * size : (k + 1) * size, :]
     size = workers_ref.shape[0] // jobs_n
     high = (messages[0].shape[0] - size) // 3
     block = jobs_ref.shape[0] // jobs_n
@@ -196,6 +176,16 @@
             start_ref[:, lanes] = value[r : r + 1, :]
             col_ref[:, lanes] = value[high // 2 + r : high // 2 + r + 1, :]
     col_ref[...] = jnp.log(col_ref[...]) - jnp.log(jnp.sum(col_ref[...], axis=1, keepdims=True))
+    worker_mass = sum(ref[high : high + high // 2, :].astype(F32) for ref in third_refs)
+    diagonal = diagonal_mask()
+    for k in range(worker_mass.shape[0]):
+        block_of_mass = jnp.where(diagonal, worker_mass[k : k + 1, :], 0.0)
+        mass_ref[k * LANES : (k + 1) * LANES, :] = jnp.broadcast_to(
+            jnp.sum(block_of_mass, axis=1, keepdims=True), (LANES, LANES)
+        )
+    log_total_ref[...] = jnp.broadcast_to(
+        jnp.log(jnp.sum(worker_mass, keepdims=True)), log_total_ref.shape
+    )
     proj_ref[...] = jnp.dot(
         workers_ref[...], affinity_ref[...], preferred_element_type=F32
     ).astype(BF16)
@@ -278,41 +268,20 @@
     def on_device(worker_feat, job_feat, affinity, worker_mass, job_mass, v_start, observed):
         rows, cols = jobs_n * worker_feat.shape[0], jobs_n * workers_n * job_feat.shape[0]
         feat = worker_feat.shape[1]
-        own_rows, own_cols = worker_feat.shape[0], cols // jobs_n
-        high = 2 * (own_cols // LANES)
+        high = 2 * (cols // jobs_n // LANES)
         wide, tall = ((1, cols + LANES), F32), ((rows, LANES), F32)
-        vmem, anywhere = pl.BlockSpec(memory_space=pltpu.VMEM), pl.BlockSpec(memory_space=pl.ANY)
-        message, mass, log_total = pl.pallas_call(
-            pack_body,
-            out_shape=(
-                jax.ShapeDtypeStruct((own_rows + 3 * high, feat), BF16),
-                jax.ShapeDtypeStruct((rows, LANES), F32),
-                jax.ShapeDtypeStruct((1, LANES), F32),
-            ),
-            in_specs=[anywhere] * 4,
-            out_specs=(vmem,) * 3,
-            scratch_shapes=[
-                pltpu.VMEM((high, LANES), F32),
-                pltpu.VMEM((rows // LANES, LANES), F32),
-                pltpu.SemaphoreType.DMA((4,)),
-            ],
-            compiler_params=pltpu.CompilerParams(vmem_limit_bytes=8 << 20),
-            name="pack",
-        )(
-            worker_feat,
-            v_start.reshape(-1, LANES),
-            job_mass.reshape(-1, LANES),
-            worker_mass.reshape(-1, LANES),
-        )
-        job_pieces = []
-        own, *others = over_job(job_feat)
-        for held in (own, jnp.concatenate(others, axis=0)):
-            across = swap(held, "worker", workers_n, 2)
-            job_pieces += [held, swap(held, "worker", workers_n, 1)]
-            job_pieces += [across, swap(across, "worker", workers_n, 1)]
+        by_lanes = [value.reshape(-1, LANES) for value in (v_start, job_mass, worker_mass)]
+        thirds = thirds_of(jnp.concatenate(by_lanes + by_lanes[-1:], axis=0))
+        message = jnp.concatenate([worker_feat] + [third[:high] for third in thirds], axis=0)
+        held = over_job(job_feat)
+        held = [held[0], held[1], jnp.concatenate(held[2:], axis=0)]
+        across = [swap(one, "worker", workers_n, 2) for one in held]
+        job_pieces = held + across
+        for pieces in (held[:1], held[1:], across[:2], across[2:]):
+            job_pieces.append(swap(jnp.concatenate(pieces, axis=0), "worker", workers_n, 1))
         messages = over_job(message)
         work = [(rows, cols), (rows, LANES), (rows, LANES)]
-        out, shift, jobs, workers, proj, log_job = call(
+        out, shift, jobs, workers, proj, log_job, mass, log_total = call(
             functools.partial(first_body, jobs_n, workers_n),
             [
                 wide,
@@ -321,10 +290,12 @@
                 ((rows, feat), BF16),
                 ((rows, feat), BF16),
                 ((1, cols), F32),
+                tall,
+                ((1, LANES), F32),
             ],
-            jobs_n + 11,
+            jobs_n + 14,
             [(1, cols)] + work,
-        )(*job_pieces, *messages, affinity, mass, log_total)
+        )(*job_pieces, *thirds, *messages, affinity)
         for _ in range(1, SWEEPS):
             out, shift = call(
                 functools.partial(next_body, workers_n),

time: 106 us -> 104 us (0.981)
  waiting for transfers between devices: 25.9 us -> 21.4 us
  starting transfers between devices: 20.9 us -> 22.5 us
    ppermute x24 -> x25, waiting for transfers between devices: 25.9 us -> 21.4 us  [swap(): return lax.ppermute(value, axis, [(i, i ^ mask) for i in range(size)])]
    ppermute x24 -> x25, starting transfers between devices: 20.9 us -> 22.5 us  [swap(): return lax.ppermute(value, axis, [(i, i ^ mask) for i in range(size)])]
  transfers between devices with their start and end apart: 24 -> 25, of which waited for: 15 -> 12; matrix products, arithmetic and copies ran while one was open for 1% -> 1% of each run, Pallas kernels for 0% -> 0%
where the time goes in v2:
time: 104 us
  Pallas kernels  56.9 us (55%)
  starting transfers between devices  22.5 us (22%)
  waiting for transfers between devices  21.4 us (21%)
  other arithmetic  1.4 us (1%)
    pallas_call x2, Pallas kernels, on_device(): call(functools.partial(next_body, workers_n), [wide, tall], workers_n + 6...  34 us
    ppermute x25, starting transfers between devices, swap(): return lax.ppermute(value, axis, [(i, i ^ mask) for i in range(size)])  22.5 us
    ppermute x25, waiting for transfers between devices, swap(): return lax.ppermute(value, axis, [(i, i ^ mask) for i in range(size)])  21.4 us
    pallas_call x1, Pallas kernels, on_device(): call(functools.partial(first_body, jobs_n, workers_n), [wide, tall, ((col...  17.6 us
    pallas_call x1, Pallas kernels, on_device(): call(functools.partial(moment_body, workers_n), [((feat, feat), F32), ((1...  5.27 us
  transfers between devices with their start and end apart: 25, of which 12 were waited for; matrix products, arithmetic and copies ran while one was open for 1% of the time, Pallas kernels for 0%

profile of v2, /device:TPU:0, one launch (start us, length us, event | category | flops | bytes accessed | tf_op | source)
XLA Modules:
  0.0 103.7 jit_solution(5574034029557874030)
XLA Ops:
  0.7 3.0 %collective-permute-start.3 = (bf16[256,128]{1,0:T(8,128)(2,1)}, bf16[256,128]{1,0:T(8,128)(2,1)S(1)}, u32[]{:S(2)}, u32[]{:S(2)}) collective-permute-start(bf16[256,128]{1,0:T(8,128)(2,1)} %refs_0_.1), channel_id=1, source_target_pairs={{0,2},{1,3},{2,0},{3,1},{4,6},{5,7},{6,4},{7,5},{8,10},{9,11},{10,... | collective-permute-start | bytes 196616 | tf_op jit(solution)/shard_map/ppermute | solution.py:22
  3.7 3.6 %collective-permute-start.2 = (bf16[256,128]{1,0:T(8,128)(2,1)}, bf16[256,128]{1,0:T(8,128)(2,1)S(1)}, u32[]{:S(2)}, u32[]{:S(2)}) collective-permute-start(bf16[256,128]{1,0:T(8,128)(2,1)} %refs_0_.1), channel_id=1, source_target_pairs={{0,12},{4,8},{8,4},{12,0},{1,13},{5,9},{9,5},{13,1},{2,14},{6,10},... | collective-permute-start | bytes 196616 | tf_op jit(solution)/shard_map/ppermute | solution.py:22
  7.3 0.0 collective-permute-start.1
  7.3 0.8 collective-permute-start
  8.1 0.0 collective-permute-start.6
  8.1 0.7 fusion.1
  8.8 4.1 %collective-permute-done.1 = bf16[256,128]{1,0:T(8,128)(2,1)S(1)} collective-permute-done((bf16[256,128]{1,0:T(8,128)(2,1)}, bf16[256,128]{1,0:T(8,128)(2,1)S(1)}, u32[]{:S(2)}, u32[]{:S(2)}) %collective-permute-start.1) | collective-permute-done | bytes 65568 | tf_op jit(solution)/shard_map/ppermute | solution.py:22
  12.9 2.5 %collective-permute-start.12 = (bf16[304,128]{1,0:T(8,128)(2,1)S(1)}, bf16[304,128]{1,0:T(8,128)(2,1)S(1)}, u32[]{:S(2)}, u32[]{:S(2)}) collective-permute-start(bf16[304,128]{1,0:T(8,128)(2,1)S(1)} %pad_maximum_fusion.2.refs_13_), channel_id=1, source_target_pairs={{0,12},{4,8},{8,4},{12,0},{1,13},{5,9},{9,5},{13,1},{2,14},{6,10},... | collective-permute-start | bytes 233480 | tf_op jit(solution)/shard_map/ppermute | solution.py:22
  15.5 0.0 collective-permute-done.2
  15.5 0.6 collective-permute-start.5
  16.1 1.5 %collective-permute-start.4 = (bf16[256,128]{1,0:T(8,128)(2,1)S(1)}, bf16[256,128]{1,0:T(8,128)(2,1)S(1)}, u32[]{:S(2)}, u32[]{:S(2)}) collective-permute-start(bf16[256,128]{1,0:T(8,128)(2,1)S(1)} %collective-permute-done.refs_1_), channel_id=1, source_target_pairs={{0,2},{1,3},{2,0},{3,1},{4,6},{5,7},{6,4},{7,5},{8,10},{9,11},{10,... | collective-permute-start | bytes 196616 | tf_op jit(solution)/shard_map/ppermute | solution.py:22
  17.6 0.0 copy-start
  17.6 0.0 copy-start.1
  17.6 0.0 collective-permute-done.3.refs_3_
  17.7 0.1 collective-permute-start.7
  17.7 3.5 %collective-permute-done.4.refs_4_ = bf16[256,128]{1,0:T(8,128)(2,1)S(1)} collective-permute-done((bf16[256,128]{1,0:T(8,128)(2,1)S(1)}, bf16[256,128]{1,0:T(8,128)(2,1)S(1)}, u32[]{:S(2)}, u32[]{:S(2)}) %collective-permute-start.4) | collective-permute-done | bytes 65568 | tf_op jit(solution)/shard_map/ppermute | solution.py:22
  21.3 0.1 collective-permute-start.8
  21.3 0.0 collective-permute-done.5.refs_5_
  21.3 0.5 collective-permute-start.9
  21.8 2.2 %collective-permute-start.10 = (bf16[304,128]{1,0:T(8,128)(2,1)S(1)}, bf16[304,128]{1,0:T(8,128)(2,1)S(1)}, u32[]{:S(2)}, u32[]{:S(2)}) collective-permute-start(bf16[304,128]{1,0:T(8,128)(2,1)S(1)} %pad_maximum_fusion.2.refs_13_), channel_id=1, source_target_pairs={{0,4},{4,0},{8,12},{12,8},{1,5},{5,1},{9,13},{13,9},{2,6},{6,2},{1... | collective-permute-start | bytes 233480 | tf_op jit(solution)/shard_map/ppermute | solution.py:22
  24.1 3.8 %collective-permute-done.11.refs_15_ = bf16[304,128]{1,0:T(8,128)(2,1)S(1)} collective-permute-done((bf16[304,128]{1,0:T(8,128)(2,1)S(1)}, bf16[304,128]{1,0:T(8,128)(2,1)S(1)}, u32[]{:S(2)}, u32[]{:S(2)}) %collective-permute-start.11) | collective-permute-done | bytes 77856 | tf_op jit(solution)/shard_map/ppermute | solution.py:22
  27.9 0.2 collective-permute-done.10.refs_14_
  28.1 17.6 %shard_map.94 = (f32[1,4224]{1,0:T(1,128)S(1)}, f32[1024,128]{1,0:T(8,128)S(1)}, bf16[4096,128]{1,0:T(8,128)(2,1)S(1)}, bf16[1024,128]{1,0:T(8,128)(2,1)S(1)}, b...) custom-call(bf16[256,128]{1,0:T(8,128)(2,1)S(1)} %copy-done, ...), custom_call_target="tpu_custom_call" | custom-call | tf_op jit(solution)/shard_map/pallas_call | solution.py:284
  45.8 0.1 collective-permute-start.15
  45.8 1.3 %collective-permute-start.14 = (f32[1,4224]{1,0:T(1,128)S(1)}, f32[1,4224]{1,0:T(1,128)S(1)}, u32[]{:S(2)}, u32[]{:S(2)}) collective-permute-start(f32[1,4224]{1,0:T(1,128)S(1)} %get-tuple-element.18.refs_0_), channel_id=1, source_target_pairs={{0,2},{1,3},{2,0},{3,1},{4,6},{5,7},{6,4},{7,5},{8,10},{9,11},{10,... | collective-permute-start | bytes 50696 | tf_op jit(solution)/shard_map/ppermute | solution.py:22
  47.1 0.6 collective-permute-start.13
  47.7 1.3 %collective-permute-done.15.refs_3_ = f32[1,4224]{1,0:T(1,128)S(1)} collective-permute-done((f32[1,4224]{1,0:T(1,128)S(1)}, f32[1,4224]{1,0:T(1,128)S(1)}, u32[]{:S(2)}, u32[]{:S(2)}) %collective-permute-start.15) | collective-permute-done | bytes 16928 | tf_op jit(solution)/shard_map/ppermute | solution.py:22
  49.0 0.6 collective-permute-done.14.refs_2_
  49.6 16.9 %shard_map.95 = (f32[1,4224]{1,0:T(1,128)S(1)}, f32[1024,128]{1,0:T(8,128)S(1)}) custom-call(f32[1,4224]{1,0:T(1,128)S(1)} %get-tuple-element.18.refs_0_, f32[1,4224]{1,0:T(1,128)S(1)} %collective-permute-done.13.refs_1_, f32[1,4224]{1,0:T(1,128)S(1)} %collective-permute-done.14.refs_2_, f32[1,4224]{1,0:T(1,128)S(1)} %collective-permute-done.15.refs_3_, ...), custom_call_target="tpu_custom_call" | custom-call | tf_op jit(solution)/shard_map/pallas_call | solution.py:300
  66.5 1.0 collective-permute-start.18
  67.5 0.5 collective-permute-start.17
  68.0 0.5 collective-permute-start.16
  68.5 1.3 %collective-permute-done.18.refs_3_ = f32[1,4224]{1,0:T(1,128)S(1)} collective-permute-done((f32[1,4224]{1,0:T(1,128)S(1)}, f32[1,4224]{1,0:T(1,128)S(1)}, u32[]{:S(2)}, u32[]{:S(2)}) %collective-permute-start.18) | collective-permute-done | bytes 16928 | tf_op jit(solution)/shard_map/ppermute | solution.py:22
  69.8 1.5 %collective-permute-done.17.refs_2_ = f32[1,4224]{1,0:T(1,128)S(1)} collective-permute-done((f32[1,4224]{1,0:T(1,128)S(1)}, f32[1,4224]{1,0:T(1,128)S(1)}, u32[]{:S(2)}, u32[]{:S(2)}) %collective-permute-start.17) | collective-permute-done | bytes 16928 | tf_op jit(solution)/shard_map/ppermute | solution.py:22
  71.3 17.1 %shard_map.96 = (f32[1,4224]{1,0:T(1,128)S(1)}, f32[1024,128]{1,0:T(8,128)S(1)}) custom-call(f32[1,4224]{1,0:T(1,128)S(1)} %get-tuple-element.25.refs_0_, f32[1,4224]{1,0:T(1,128)S(1)} %collective-permute-done.16.refs_1_, f32[1,4224]{1,0:T(1,128)S(1)} %collective-permute-done.17.refs_2_, f32[1,4224]{1,0:T(1,128)S(1)} %collective-permute-done.18.refs_3_, ...), custom_call_target="tpu_custom_call" | custom-call | tf_op jit(solution)/shard_map/pallas_call | solution.py:300
  88.4 0.1 collective-permute-start.21
  88.5 1.0 collective-permute-start.20
  89.4 0.9 collective-permute-start.19
  90.3 1.3 %collective-permute-done.21.refs_3_ = f32[1,4224]{1,0:T(1,128)S(1)} collective-permute-done((f32[1,4224]{1,0:T(1,128)S(1)}, f32[1,4224]{1,0:T(1,128)S(1)}, u32[]{:S(2)}, u32[]{:S(2)}) %collective-permute-start.21) | collective-permute-done | bytes 16928 | tf_op jit(solution)/shard_map/ppermute | solution.py:22
  91.6 0.7 collective-permute-done.20.refs_2_
  92.3 5.3 %shard_map.97 = (f32[128,128]{1,0:T(8,128)S(1)}, f32[1,1024]{1,0:T(1,128)}, f32[1,4096]{1,0:T(1,128)S(1)}) custom-call(f32[1,4224]{1,0:T(1,128)S(1)} %get-tuple-element.27.refs_0_, f32[1,4224]{1,0:T(1,128)S(1)} %collective-permute-done.19.refs_1_, f32[1,4224]{1,0:T(1,128)S(1)} %collective-permute-done.20.refs_2_, ...), custom_call_target="tpu_custom_call" | custom-call | tf_op jit(solution)/shard_map/pallas_call | solution.py:307
  97.5 0.6 collective-permute-start.24
  98.2 0.5 collective-permute-start.23
  98.7 0.7 collective-permute-start.22
  99.4 0.6 slice.15
  100.0 1.6 %collective-permute-done.24 = f32[128,128]{1,0:T(8,128)S(1)} collective-permute-done((f32[128,128]{1,0:T(8,128)S(1)}, f32[128,128]{1,0:T(8,128)S(1)}, u32[]{:S(2)}, u32[]{:S(2)}) %collective-permute-start.24) | collective-permute-done | bytes 65568 | tf_op jit(solution)/shard_map/ppermute | solution.py:22
  101.6 1.4 %collective-permute-done.23 = f32[128,128]{1,0:T(8,128)S(1)} collective-permute-done((f32[128,128]{1,0:T(8,128)S(1)}, f32[128,128]{1,0:T(8,128)S(1)}, u32[]{:S(2)}, u32[]{:S(2)}) %collective-permute-start.23) | collective-permute-done | bytes 65568 | tf_op jit(solution)/shard_map/ppermute | solution.py:22
  103.0 0.7 add_subtract_fusion
  (27 shorter events, 0.1 us)
Async XLA Ops:
  0.6 7.4 %copy-start.4 = (f32[1024]{0:T(1024)S(1)}, f32[1024]{0:T(1024)}, u32[]{:S(2)}) copy-start(f32[1024]{0:T(1024)} %param.10) | copy-start | bytes 12292
  0.6 8.2 %copy-start.2 = (bf16[256,128]{1,0:T(8,128)(2,1)S(1)}, bf16[256,128]{1,0:T(8,128)(2,1)}, u32[]{:S(2)}) copy-start(bf16[256,128]{1,0:T(8,128)(2,1)} %param.7) | copy-start | bytes 196612
  0.7 17.0 %collective-permute-start.3 = (bf16[256,128]{1,0:T(8,128)(2,1)}, bf16[256,128]{1,0:T(8,128)(2,1)S(1)}, u32[]{:S(2)}, u32[]{:S(2)}) collective-permute-start(bf16[256,128]{1,0:T(8,128)(2,1)} %refs_0_.1), channel_id=1, source_target_pairs={{0,2},{1,3},{2,0},{3,1},{4,6},{5,7},{6,4},{7,5},{8,10},{9,11},{10,... | collective-permute-start | bytes 196616 | tf_op jit(solution)/shard_map/ppermute | solution.py:22
  3.7 11.8 %collective-permute-start.2 = (bf16[256,128]{1,0:T(8,128)(2,1)}, bf16[256,128]{1,0:T(8,128)(2,1)S(1)}, u32[]{:S(2)}, u32[]{:S(2)}) collective-permute-start(bf16[256,128]{1,0:T(8,128)(2,1)} %refs_0_.1), channel_id=1, source_target_pairs={{0,12},{4,8},{8,4},{12,0},{1,13},{5,9},{9,5},{13,1},{2,14},{6,10},... | collective-permute-start | bytes 196616 | tf_op jit(solution)/shard_map/ppermute | solution.py:22
  7.3 5.7 %collective-permute-start.1 = (bf16[256,128]{1,0:T(8,128)(2,1)}, bf16[256,128]{1,0:T(8,128)(2,1)S(1)}, u32[]{:S(2)}, u32[]{:S(2)}) collective-permute-start(bf16[256,128]{1,0:T(8,128)(2,1)} %refs_0_.1), channel_id=1, source_target_pairs={{0,8},{4,12},{8,0},{12,4},{1,9},{5,13},{9,1},{13,5},{2,10},{6,14},... | collective-permute-start | bytes 196616 | tf_op jit(solution)/shard_map/ppermute | solution.py:22
  7.3 8.8 %collective-permute-start = (bf16[256,128]{1,0:T(8,128)(2,1)}, bf16[256,128]{1,0:T(8,128)(2,1)S(1)}, u32[]{:S(2)}, u32[]{:S(2)}) collective-permute-start(bf16[256,128]{1,0:T(8,128)(2,1)} %refs_0_.1), channel_id=1, source_target_pairs={{0,4},{4,0},{8,12},{12,8},{1,5},{5,1},{9,13},{13,9},{2,6},{6,2},{1... | collective-permute-start | bytes 196616 | tf_op jit(solution)/shard_map/ppermute | solution.py:22
  8.1 13.8 %collective-permute-start.6 = (bf16[256,128]{1,0:T(8,128)(2,1)}, bf16[256,128]{1,0:T(8,128)(2,1)S(1)}, u32[]{:S(2)}, u32[]{:S(2)}) collective-permute-start(bf16[256,128]{1,0:T(8,128)(2,1)} %refs_0_.1), channel_id=1, source_target_pairs={{0,1},{1,0},{2,3},{3,2},{4,5},{5,4},{6,7},{7,6},{8,9},{9,8},{10,11... | collective-permute-start | bytes 196616 | tf_op jit(solution)/shard_map/ppermute | solution.py:22
  12.9 8.9 %collective-permute-start.12 = (bf16[304,128]{1,0:T(8,128)(2,1)S(1)}, bf16[304,128]{1,0:T(8,128)(2,1)S(1)}, u32[]{:S(2)}, u32[]{:S(2)}) collective-permute-start(bf16[304,128]{1,0:T(8,128)(2,1)S(1)} %pad_maximum_fusion.2.refs_13_), channel_id=1, source_target_pairs={{0,12},{4,8},{8,4},{12,0},{1,13},{5,9},{9,5},{13,1},{2,14},{6,10},... | collective-permute-start | bytes 233480 | tf_op jit(solution)/shard_map/ppermute | solution.py:22
  15.5 5.8 %collective-permute-start.5 = (bf16[512,128]{1,0:T(8,128)(2,1)S(1)}, bf16[512,128]{1,0:T(8,128)(2,1)S(1)}, u32[]{:S(2)}, u32[]{:S(2)}) collective-permute-start(bf16[512,128]{1,0:T(8,128)(2,1)S(1)} %constant_dynamic-update-slice_fusion.refs_2_), channel_id=1, source_target_pairs={{0,2},{1,3},{2,0},{3,1},{4,6},{5,7},{6,4},{7,5},{8,10},{9,11},{10,... | collective-permute-start | bytes 393224 | tf_op jit(solution)/shard_map/ppermute | solution.py:22
  16.1 5.1 %collective-permute-start.4 = (bf16[256,128]{1,0:T(8,128)(2,1)S(1)}, bf16[256,128]{1,0:T(8,128)(2,1)S(1)}, u32[]{:S(2)}, u32[]{:S(2)}) collective-permute-start(bf16[256,128]{1,0:T(8,128)(2,1)S(1)} %collective-permute-done.refs_1_), channel_id=1, source_target_pairs={{0,2},{1,3},{2,0},{3,1},{4,6},{5,7},{6,4},{7,5},{8,10},{9,11},{10,... | collective-permute-start | bytes 196616 | tf_op jit(solution)/shard_map/ppermute | solution.py:22
  17.6 10.5 %copy-start = (bf16[256,128]{1,0:T(8,128)(2,1)S(1)}, bf16[256,128]{1,0:T(8,128)(2,1)}, u32[]{:S(2)}) copy-start(bf16[256,128]{1,0:T(8,128)(2,1)} %refs_0_.1) | copy-start | bytes 196612
  17.6 10.5 %copy-start.1 = (bf16[128,128]{1,0:T(8,128)(2,1)S(1)}, bf16[128,128]{1,0:T(8,128)(2,1)}, u32[]{:S(2)}) copy-start(bf16[128,128]{1,0:T(8,128)(2,1)} %refs_17_.1) | copy-start | bytes 98308
  17.7 10.4 %collective-permute-start.7 = (bf16[768,128]{1,0:T(8,128)(2,1)S(1)}, bf16[768,128]{1,0:T(8,128)(2,1)S(1)}, u32[]{:S(2)}, u32[]{:S(2)}) collective-permute-start(bf16[768,128]{1,0:T(8,128)(2,1)S(1)} %pad_maximum_fusion), channel_id=1, source_target_pairs={{0,1},{1,0},{2,3},{3,2},{4,5},{5,4},{6,7},{7,6},{8,9},{9,8},{10,11... | collective-permute-start | bytes 589832 | tf_op jit(solution)/shard_map/ppermute | solution.py:22
  21.3 6.8 %collective-permute-start.8 = (bf16[512,128]{1,0:T(8,128)(2,1)S(1)}, bf16[512,128]{1,0:T(8,128)(2,1)S(1)}, u32[]{:S(2)}, u32[]{:S(2)}) collective-permute-start(bf16[512,128]{1,0:T(8,128)(2,1)S(1)} %pad_maximum_fusion.1), channel_id=1, source_target_pairs={{0,1},{1,0},{2,3},{3,2},{4,5},{5,4},{6,7},{7,6},{8,9},{9,8},{10,11... | collective-permute-start | bytes 393224 | tf_op jit(solution)/shard_map/ppermute | solution.py:22
  21.3 6.8 %collective-permute-start.9 = (bf16[512,128]{1,0:T(8,128)(2,1)S(1)}, bf16[512,128]{1,0:T(8,128)(2,1)S(1)}, u32[]{:S(2)}, u32[]{:S(2)}) collective-permute-start(bf16[512,128]{1,0:T(8,128)(2,1)S(1)} %collective-permute-done.5.refs_5_), channel_id=1, source_target_pairs={{0,1},{1,0},{2,3},{3,2},{4,5},{5,4},{6,7},{7,6},{8,9},{9,8},{10,11... | collective-permute-start | bytes 393224 | tf_op jit(solution)/shard_map/ppermute | solution.py:22
  21.8 6.0 %collective-permute-start.11 = (bf16[304,128]{1,0:T(8,128)(2,1)S(1)}, bf16[304,128]{1,0:T(8,128)(2,1)S(1)}, u32[]{:S(2)}, u32[]{:S(2)}) collective-permute-start(bf16[304,128]{1,0:T(8,128)(2,1)S(1)} %pad_maximum_fusion.2.refs_13_), channel_id=1, source_target_pairs={{0,8},{4,12},{8,0},{12,4},{1,9},{5,13},{9,1},{13,5},{2,10},{6,14},... | collective-permute-start | bytes 233480 | tf_op jit(solution)/shard_map/ppermute | solution.py:22
  21.8 6.2 %collective-permute-start.10 = (bf16[304,128]{1,0:T(8,128)(2,1)S(1)}, bf16[304,128]{1,0:T(8,128)(2,1)S(1)}, u32[]{:S(2)}, u32[]{:S(2)}) collective-permute-start(bf16[304,128]{1,0:T(8,128)(2,1)S(1)} %pad_maximum_fusion.2.refs_13_), channel_id=1, source_target_pairs={{0,4},{4,0},{8,12},{12,8},{1,5},{5,1},{9,13},{13,9},{2,6},{6,2},{1... | collective-permute-start | bytes 233480 | tf_op jit(solution)/shard_map/ppermute | solution.py:22
  45.8 3.2 %collective-permute-start.15 = (f32[1,4224]{1,0:T(1,128)S(1)}, f32[1,4224]{1,0:T(1,128)S(1)}, u32[]{:S(2)}, u32[]{:S(2)}) collective-permute-start(f32[1,4224]{1,0:T(1,128)S(1)} %get-tuple-element.18.refs_0_), channel_id=1, source_target_pairs={{0,3},{1,2},{2,1},{3,0},{4,7},{5,6},{6,5},{7,4},{8,11},{9,10},{10,... | collective-permute-start | bytes 50696 | tf_op jit(solution)/shard_map/ppermute | solution.py:22
  45.8 3.8 %collective-permute-start.14 = (f32[1,4224]{1,0:T(1,128)S(1)}, f32[1,4224]{1,0:T(1,128)S(1)}, u32[]{:S(2)}, u32[]{:S(2)}) collective-permute-start(f32[1,4224]{1,0:T(1,128)S(1)} %get-tuple-element.18.refs_0_), channel_id=1, source_target_pairs={{0,2},{1,3},{2,0},{3,1},{4,6},{5,7},{6,4},{7,5},{8,10},{9,11},{10,... | collective-permute-start | bytes 50696 | tf_op jit(solution)/shard_map/ppermute | solution.py:22
  47.1 2.5 %collective-permute-start.13 = (f32[1,4224]{1,0:T(1,128)S(1)}, f32[1,4224]{1,0:T(1,128)S(1)}, u32[]{:S(2)}, u32[]{:S(2)}) collective-permute-start(f32[1,4224]{1,0:T(1,128)S(1)} %get-tuple-element.18.refs_0_), channel_id=1, source_target_pairs={{0,1},{1,0},{2,3},{3,2},{4,5},{5,4},{6,7},{7,6},{8,9},{9,8},{10,11... | collective-permute-start | bytes 50696 | tf_op jit(solution)/shard_map/ppermute | solution.py:22
  66.5 3.2 %collective-permute-start.18 = (f32[1,4224]{1,0:T(1,128)S(1)}, f32[1,4224]{1,0:T(1,128)S(1)}, u32[]{:S(2)}, u32[]{:S(2)}) collective-permute-start(f32[1,4224]{1,0:T(1,128)S(1)} %get-tuple-element.25.refs_0_), channel_id=1, source_target_pairs={{0,3},{1,2},{2,1},{3,0},{4,7},{5,6},{6,5},{7,4},{8,11},{9,10},{10,... | collective-permute-start | bytes 50696 | tf_op jit(solution)/shard_map/ppermute | solution.py:22
  67.5 3.7 %collective-permute-start.17 = (f32[1,4224]{1,0:T(1,128)S(1)}, f32[1,4224]{1,0:T(1,128)S(1)}, u32[]{:S(2)}, u32[]{:S(2)}) collective-permute-start(f32[1,4224]{1,0:T(1,128)S(1)} %get-tuple-element.25.refs_0_), channel_id=1, source_target_pairs={{0,2},{1,3},{2,0},{3,1},{4,6},{5,7},{6,4},{7,5},{8,10},{9,11},{10,... | collective-permute-start | bytes 50696 | tf_op jit(solution)/shard_map/ppermute | solution.py:22
  68.0 3.3 %collective-permute-start.16 = (f32[1,4224]{1,0:T(1,128)S(1)}, f32[1,4224]{1,0:T(1,128)S(1)}, u32[]{:S(2)}, u32[]{:S(2)}) collective-permute-start(f32[1,4224]{1,0:T(1,128)S(1)} %get-tuple-element.25.refs_0_), channel_id=1, source_target_pairs={{0,1},{1,0},{2,3},{3,2},{4,5},{5,4},{6,7},{7,6},{8,9},{9,8},{10,11... | collective-permute-start | bytes 50696 | tf_op jit(solution)/shard_map/ppermute | solution.py:22
  88.4 3.2 %collective-permute-start.21 = (f32[1,4224]{1,0:T(1,128)S(1)}, f32[1,4224]{1,0:T(1,128)S(1)}, u32[]{:S(2)}, u32[]{:S(2)}) collective-permute-start(f32[1,4224]{1,0:T(1,128)S(1)} %get-tuple-element.27.refs_0_), channel_id=1, source_target_pairs={{0,3},{1,2},{2,1},{3,0},{4,7},{5,6},{6,5},{7,4},{8,11},{9,10},{10,... | collective-permute-start | bytes 50696 | tf_op jit(solution)/shard_map/ppermute | solution.py:22
  88.5 3.8 %collective-permute-start.20 = (f32[1,4224]{1,0:T(1,128)S(1)}, f32[1,4224]{1,0:T(1,128)S(1)}, u32[]{:S(2)}, u32[]{:S(2)}) collective-permute-start(f32[1,4224]{1,0:T(1,128)S(1)} %get-tuple-element.27.refs_0_), channel_id=1, source_target_pairs={{0,2},{1,3},{2,0},{3,1},{4,6},{5,7},{6,4},{7,5},{8,10},{9,11},{10,... | collective-permute-start | bytes 50696 | tf_op jit(solution)/shard_map/ppermute | solution.py:22
  89.4 2.8 %collective-permute-start.19 = (f32[1,4224]{1,0:T(1,128)S(1)}, f32[1,4224]{1,0:T(1,128)S(1)}, u32[]{:S(2)}, u32[]{:S(2)}) collective-permute-start(f32[1,4224]{1,0:T(1,128)S(1)} %get-tuple-element.27.refs_0_), channel_id=1, source_target_pairs={{0,1},{1,0},{2,3},{3,2},{4,5},{5,4},{6,7},{7,6},{8,9},{9,8},{10,11... | collective-permute-start | bytes 50696 | tf_op jit(solution)/shard_map/ppermute | solution.py:22
  92.3 10.7 %copy-start.3 = (f32[128,128]{1,0:T(8,128)S(1)}, f32[128,128]{1,0:T(8,128)}, u32[]{:S(2)}) copy-start(f32[128,128]{1,0:T(8,128)} %param.13) | copy-start | bytes 196612
  97.5 4.1 %collective-permute-start.24 = (f32[128,128]{1,0:T(8,128)S(1)}, f32[128,128]{1,0:T(8,128)S(1)}, u32[]{:S(2)}, u32[]{:S(2)}) collective-permute-start(f32[128,128]{1,0:T(8,128)S(1)} %get-tuple-element.30), channel_id=1, source_target_pairs={{0,3},{1,2},{2,1},{3,0},{4,7},{5,6},{6,5},{7,4},{8,11},{9,10},{10,... | collective-permute-start | bytes 196616 | tf_op jit(solution)/shard_map/ppermute | solution.py:22
  98.2 4.8 %collective-permute-start.23 = (f32[128,128]{1,0:T(8,128)S(1)}, f32[128,128]{1,0:T(8,128)S(1)}, u32[]{:S(2)}, u32[]{:S(2)}) collective-permute-start(f32[128,128]{1,0:T(8,128)S(1)} %get-tuple-element.30), channel_id=1, source_target_pairs={{0,2},{1,3},{2,0},{3,1},{4,6},{5,7},{6,4},{7,5},{8,10},{9,11},{10,... | collective-permute-start | bytes 196616 | tf_op jit(solution)/shard_map/ppermute | solution.py:22
  98.7 4.3 %collective-permute-start.22 = (f32[128,128]{1,0:T(8,128)S(1)}, f32[128,128]{1,0:T(8,128)S(1)}, u32[]{:S(2)}, u32[]{:S(2)}) collective-permute-start(f32[128,128]{1,0:T(8,128)S(1)} %get-tuple-element.30), channel_id=1, source_target_pairs={{0,1},{1,0},{2,3},{3,2},{4,5},{5,4},{6,7},{7,6},{8,9},{9,8},{10,11... | collective-permute-start | bytes 196616 | tf_op jit(solution)/shard_map/ppermute | solution.py:22
